TPU v7x, 256 devices: a whole 4x4x8 slice. The times are simulated.
256 devices in a mesh: lon: 32 (over y, z), lat: 8 (over x, core).
Axes of the slice: x: 4, y: 4, z: 8, core: 2. Of those that a mesh axis runs over, the one named last changes fastest.
Arguments:
- fields: float32 [129, 6, 128, 1024], P(None, None, 'lat', 'lon'), may hold values from -38 to 38
Outputs:
- koopman_modes: float32 [30, 128, 1024, 128], P(None, 'lat', 'lon')
- forward_operator: float32 [128, 128], replicated
- backward_operator: float32 [128, 128], replicated
All inputs are finite; a program needn't handle non-finite values.
Results may differ from a plain program's by a relative error of at most 0.0001.
Values sent between devices are 32-bit elements; how exact they have to be, the bound alone decides.
A program may use at most 64 MiB of HBM per device.

v0:
```python
import jax
import jax.numpy as jnp
from jax import lax
from jax.sharding import PartitionSpec as P


def with_halo(block, sides, width, periodic):
    for axis, dim in sides:
        count = lax.axis_size(axis)
        forward = [(i, i + 1) for i in range(count - 1)]
        if periodic:
            forward.append((count - 1, 0))
        backward = [(target, source) for source, target in forward]
        low = lax.ppermute(
            lax.slice_in_dim(block, block.shape[dim] - width, None, axis=dim), axis, forward
        )
        high = lax.ppermute(lax.slice_in_dim(block, 0, width, axis=dim), axis, backward)
        block = jnp.concatenate([low, block, high], axis=dim)
    return block


def reduced_operators(upper_factor, gram_total):
    snap_count = upper_factor.shape[0] - 1
    head_block = upper_factor[:snap_count, :snap_count]
    forward_operator = jax.scipy.linalg.solve_triangular(
        head_block.T, upper_factor[:snap_count, 1:].T, lower=True
    ).T
    back_factor = jnp.linalg.cholesky(gram_total[1:, 1:])
    mixed_block = jax.scipy.linalg.solve_triangular(
        back_factor, gram_total[1:, :snap_count], lower=True
    )
    backward_operator = jax.scipy.linalg.solve_triangular(back_factor, mixed_block.T, lower=True).T
    return (forward_operator, backward_operator)


def shards(fields):
    states = fields.shape[0]
    snap_count = states - 1
    channels = fields.shape[1]
    band_rows = fields.shape[2]
    sector_cols = fields.shape[3]
    lon_padded = with_halo(fields, (("lon", 3),), 1, True)
    lat_padded = with_halo(fields, (("lat", 2),), 1, False)
    neighbour_list = (
        lat_padded[:, :, :-2],
        lat_padded[:, :, 2:],
        lon_padded[:, :, :, :-2],
        lon_padded[:, :, :, 2:],
    )
    slab_list = [fields] + [fields * neighbour for neighbour in neighbour_list]
    rows_total = (
        5 * channels * band_rows * lax.axis_size("lat") * sector_cols * lax.axis_size("lon")
    )
    gram_local = jnp.zeros((states, states), jnp.float32)
    for feature_slab in slab_list:
        flat_rows = feature_slab.reshape(states, -1)
        gram_local = gram_local + jnp.dot(flat_rows, flat_rows.T, precision=lax.Precision.HIGHEST)
    gram_local = gram_local / rows_total
    gram_total = lax.psum(gram_local, ("lon", "lat"))
    upper_factor = jnp.linalg.cholesky(gram_total).T
    forward_operator, backward_operator = reduced_operators(upper_factor, gram_total)
    head_block = upper_factor[:snap_count, :snap_count]
    mode_parts = []
    for feature_slab in slab_list:
        flat_rows = feature_slab.reshape(states, -1)[:snap_count]
        solved = jax.scipy.linalg.solve_triangular(head_block.T, flat_rows, lower=True)
        mode_parts.append(
            solved.reshape(snap_count, channels, band_rows, sector_cols).transpose(1, 2, 3, 0)
        )
    koopman_modes = jnp.concatenate(mode_parts, axis=0)
    return (koopman_modes, forward_operator, backward_operator)


def solution(mesh):
    placed = (P(None, None, "lat", "lon"),)
    return jax.shard_map(
        shards,
        mesh=mesh,
        in_specs=placed,
        out_specs=(P(None, "lat", "lon", None), P(), P()),
        check_vma=False,
    )
```

profile of v0, /device:TPU:1, one launch (start us, length us, event | category | flops | bytes accessed | tf_op | source)
XLA Modules:
  0.0 389.0 jit_solution(6079797568631075508)
XLA Ops:
  7.2 1.5 fusion.35
  8.8 8.9 %collective-permute-start.3 = (f32[129,6,16,1]{0,2,3,1:T(8,128)S(1)}, f32[129,6,16,1]{0,2,3,1:T(8,128)S(1)}, u32[]{:S(2)}, u32[]{:S(2)}) collective-permute-start(f32[129,6,16,1]{0,2,3,1:T(8,128)S(1)} %copy.74), channel_id=1, source_target_pairs={{8,0},{16,8},{24,16},{32,24},{40,32},{48,40},{56,48},{64,56},{72,6... | collective-permute-start | bytes 148616 | tf_op jit(solution)/shard_map/ppermute | solution.py:17
  18.8 4.0 %collective-permute-start = (f32[129,6,1,32]{0,3,2,1:T(8,128)S(1)}, f32[129,6,1,32]{0,3,2,1:T(8,128)S(1)}, u32[]{:S(2)}, u32[]{:S(2)}) collective-permute-start(f32[129,6,1,32]{0,3,2,1:T(8,128)S(1)} %get-tuple-element.18), channel_id=1, source_target_pairs={{0,1},{1,2},{2,3},{3,4},{4,5},{5,6},{6,7},{8,9},{9,10},{10,11},{11... | collective-permute-start | bytes 297224 | tf_op jit(solution)/shard_map/ppermute | solution.py:14
  22.8 2.2 collective-permute-start.1
  25.0 8.0 %convolution_bitcast_fusion.4 = f32[129,129]{0,1:T(8,128)S(1)} fusion(f32[129,6,16,32]{0,3,2,1:T(8,128)} %param.5), kind=kOutput, calls=%fused_computation.12 | convolution fusion | flops 613453824 | bytes 1651716 | tf_op jit(solution)/shard_map/dot_general | solution.py:57
  33.3 2.8 fusion.3
  36.1 5.1 %convolution_bitcast_fusion.2 = f32[129,129]{0,1:T(8,128)S(1)} fusion(f32[129,6,16,32]{0,3,2,1:T(8,128)S(1)} %get-tuple-element.15), kind=kOutput, calls=%fused_computation.10 | convolution fusion | flops 613453824 | bytes 1651716 | tf_op jit(solution)/shard_map/dot_general | solution.py:57
  41.3 5.1 %convolution_bitcast_fusion.1 = f32[129,129]{0,1:T(8,128)S(1)} fusion(f32[129,6,16,32]{0,3,2,1:T(8,128)S(1)} %get-tuple-element.16), kind=kOutput, calls=%fused_computation.9 | convolution fusion | flops 613453824 | bytes 1651716 | tf_op jit(solution)/shard_map/dot_general | solution.py:57
  46.4 5.3 %convolution_bitcast_fusion = f32[129,129]{0,1:T(8,128)S(1)} fusion(f32[129,6,16,32]{0,3,2,1:T(8,128)S(1)} %get-tuple-element.17), kind=kOutput, calls=%fused_computation.8 | convolution fusion | flops 613453824 | bytes 1651716 | tf_op jit(solution)/shard_map/dot_general | solution.py:57
  51.8 5.8 %fusion.8 = f32[129,129]{0,1:T(8,128)} fusion(f32[129,129]{0,1:T(8,128)S(1)} %convolution_bitcast_fusion, f32[129,129]{0,1:T(8,128)S(1)} %convolution_bitcast_fusion.1, f32[129,129]{0,1:T(8,128)S(1)} %convolution_bitcast_fusion.2, f32[129,129]{0,1:T(8,128)S(1)} %convolution_bitcast_fusion.4, f32[129,6,16,32]{0,3,2,1:T(8,128)S(1)} %get-tuple-element.14), kind=kOutput, calls=%fused_computation.17 | convolution fusion | flops 613537024 | bytes 1917972 | tf_op jit(solution)/shard_map/dot_general | solution.py:57
  57.6 1.7 slice.141
  60.9 1.3 slice.143
  63.6 239.0 %all-reduce.3.cloned.1.call-done = f32[129,129]{0,1:T(8,128)} async-done(((f32[129,129]{0,1:T(8,128)}), f32[129,129]{0,1:T(8,128)}) %all-reduce.3.cloned.1.call-update) | async-done | bytes 66580 | tf_op jit(solution)/shard_map/psum | solution.py:59
  307.2 11.7 %cholesky.144 = f32[128,128]{1,0:T(8,128)S(1)} custom-call(f32[128,128]{1,0:T(8,128)S(1)} %fusion.16), custom_call_target="Cholesky" | custom-call | tf_op jit(solution)/shard_map/jit(cholesky)/cholesky | solution.py:28
  320.2 10.0 %custom-call.31 = f32[1,128,128]{1,2,0:T(8,128)S(1)} custom-call(f32[1,128,128]{2,1,0:T(8,128)S(1)} %fusion.10), custom_call_target="InvertDiagBlocksLowerTriangular" | custom-call | tf_op jit(solution)/shard_map/jit(_solve_triangular)/triangular_solve | solution.py:32
  332.6 11.7 %cholesky.63 = f32[128,128]{1,0:T(8,128)S(1)} custom-call(f32[128,128]{1,0:T(8,128)S(1)} %copy.46), custom_call_target="Cholesky" | custom-call | tf_op jit(solution)/shard_map/jit(cholesky)/cholesky | solution.py:60
  345.1 9.8 %custom-call.17 = f32[1,128,128]{1,2,0:T(8,128)S(1)} custom-call(f32[1,128,128]{2,1,0:T(8,128)S(1)} %get-tuple-element.23), custom_call_target="InvertDiagBlocksLowerTriangular" | custom-call | tf_op jit(solution)/shard_map/jit(cholesky)/cholesky | solution.py:60
  358.2 9.8 %custom-call.24 = f32[1,128,128]{1,2,0:T(8,128)S(1)} custom-call(f32[1,128,128]{2,1,0:T(8,128)S(1)} %fusion.13), custom_call_target="InvertDiagBlocksLowerTriangular" | custom-call | tf_op jit(solution)/shard_map/jit(_solve_triangular)/triangular_solve | solution.py:66
  369.0 2.8 fusion.24
  371.9 1.4 fusion.22
  373.3 1.4 fusion.20
  374.6 1.4 fusion.18
  376.0 1.4 fusion.26
  378.5 3.2 copy-done.9
  (65 shorter events, 16.8 us)
Async XLA Ops:
  7.2 295.4 %all-reduce.3.cloned.1.call-start = ((), (), s32[]{:S(2)}) async-start(), calls=%async_computation | async-start | bytes 278528 | tf_op jit(solution)/shard_map/psum | solution.py:59
  8.8 24.3 %collective-permute-start.3 = (f32[129,6,16,1]{0,2,3,1:T(8,128)S(1)}, f32[129,6,16,1]{0,2,3,1:T(8,128)S(1)}, u32[]{:S(2)}, u32[]{:S(2)}) collective-permute-start(f32[129,6,16,1]{0,2,3,1:T(8,128)S(1)} %copy.74), channel_id=1, source_target_pairs={{8,0},{16,8},{24,16},{32,24},{40,32},{48,40},{56,48},{64,56},{72,6... | collective-permute-start | bytes 148616 | tf_op jit(solution)/shard_map/ppermute | solution.py:17
  17.7 15.4 %collective-permute-start.2 = (f32[129,6,16,1]{0,2,3,1:T(8,128)S(1)}, f32[129,6,16,1]{0,2,3,1:T(8,128)S(1)}, u32[]{:S(2)}, u32[]{:S(2)}) collective-permute-start(f32[129,6,16,1]{0,2,3,1:T(8,128)S(1)} %copy.73), channel_id=1, source_target_pairs={{0,8},{8,16},{16,24},{24,32},{32,40},{40,48},{48,56},{56,64},{64,7... | collective-permute-start | bytes 148616 | tf_op jit(solution)/shard_map/ppermute | solution.py:14
  18.8 14.4 %collective-permute-start = (f32[129,6,1,32]{0,3,2,1:T(8,128)S(1)}, f32[129,6,1,32]{0,3,2,1:T(8,128)S(1)}, u32[]{:S(2)}, u32[]{:S(2)}) collective-permute-start(f32[129,6,1,32]{0,3,2,1:T(8,128)S(1)} %get-tuple-element.18), channel_id=1, source_target_pairs={{0,1},{1,2},{2,3},{3,4},{4,5},{5,6},{6,7},{8,9},{9,10},{10,11},{11... | collective-permute-start | bytes 297224 | tf_op jit(solution)/shard_map/ppermute | solution.py:14
  22.8 10.5 %copy-start = (f32[129,6,16,32]{0,3,2,1:T(8,128)S(1)}, f32[129,6,16,32]{0,3,2,1:T(8,128)}, u32[]{:S(2)}) copy-start(f32[129,6,16,32]{0,3,2,1:T(8,128)} %param.5) | copy-start | bytes 4755460
  22.8 10.4 %collective-permute-start.1 = (f32[129,6,1,32]{0,3,2,1:T(8,128)S(1)}, f32[129,6,1,32]{0,3,2,1:T(8,128)S(1)}, u32[]{:S(2)}, u32[]{:S(2)}) collective-permute-start(f32[129,6,1,32]{0,3,2,1:T(8,128)S(1)} %get-tuple-element.19), channel_id=1, source_target_pairs={{1,0},{2,1},{3,2},{4,3},{5,4},{6,5},{7,6},{9,8},{10,9},{11,10},{12... | collective-permute-start | bytes 297224 | tf_op jit(solution)/shard_map/ppermute | solution.py:17
  36.1 5.2 %copy-start.3 = (f32[129,6,16,32]{0,3,2,1:T(8,128)}, f32[129,6,16,32]{0,3,2,1:T(8,128)S(1)}, u32[]{:S(2)}) copy-start(f32[129,6,16,32]{0,3,2,1:T(8,128)S(1)} %get-tuple-element.16) | copy-start | bytes 4755460
  36.1 10.3 %copy-start.1 = (f32[129,6,16,32]{0,3,2,1:T(8,128)}, f32[129,6,16,32]{0,3,2,1:T(8,128)S(1)}, u32[]{:S(2)}) copy-start(f32[129,6,16,32]{0,3,2,1:T(8,128)S(1)} %get-tuple-element.17) | copy-start | bytes 4755460
  36.1 15.7 %copy-start.5 = (f32[129,6,16,32]{0,3,2,1:T(8,128)}, f32[129,6,16,32]{0,3,2,1:T(8,128)S(1)}, u32[]{:S(2)}) copy-start(f32[129,6,16,32]{0,3,2,1:T(8,128)S(1)} %get-tuple-element.15) | copy-start | bytes 4755460
  36.1 15.7 %copy-start.6 = (f32[129,6,16,32]{0,3,2,1:T(8,128)}, f32[129,6,16,32]{0,3,2,1:T(8,128)S(1)}, u32[]{:S(2)}) copy-start(f32[129,6,16,32]{0,3,2,1:T(8,128)S(1)} %get-tuple-element.14) | copy-start | bytes 4755460
  57.6 2.4 copy-start.4
  57.6 3.3 copy-start.2
  60.0 2.3 copy-start.7
  371.8 2.8 copy-start.8
  373.2 2.8 slice-start
  378.5 3.2 copy-start.9
Sparse Core Ops, SparseCore 0:
  57.7 244.7 all-reduce.2
where the time goes:
time: 395 us; the launch traced here: 389 us
  waiting for transfers between devices  239 us (61%)
  other arithmetic  59.8 us (15%)
  matrix products  40.3 us (10%)
  local copies, waits for them, and re-layouts  17.8 us (5%)
  between operations  16.9 us (4%)
  starting transfers between devices  15.2 us (4%)
    psum x1, waiting for transfers between devices, shards(): gram_total = lax.psum(gram_local, ('lon', 'lat'))  239 us
    dot_general x5, matrix products, shards(): jnp.dot(flat_rows, flat_rows.T, precision=lax.Precision.HIGHEST)  29.4 us
    another operation x4, other arithmetic, shards(): upper_factor = jnp.linalg.cholesky(gram_total).T  22.3 us
    another operation x3, other arithmetic, reduced_operators(): back_factor = jnp.linalg.cholesky(gram_total[1:, 1:])  12.4 us
    ppermute x2, starting transfers between devices, with_halo(): lax.ppermute(lax.slice_in_dim(block, 0, width, axis=dim), axis, backward)  11.1 us
    another operation x2, other arithmetic, reduced_operators(): jax.scipy.linalg.solve_triangular(back_factor, mixed_block.T, lower=True)  10.6 us
    another operation x2, other arithmetic, shards(): jax.scipy.linalg.solve_triangular(head_block.T, flat_rows, lower=True)  9.82 us
    another operation x5, matrix products, shards(): jax.scipy.linalg.solve_triangular(head_block.T, flat_rows, lower=True)  8.3 us
  transfers between devices with their start and end apart: 5, of which 1 were waited for; matrix products, arithmetic and copies ran while one was open for 4% of the time, Pallas kernels for 0%

commit v1 on v0

v1 whole, which is shorter than its diff:
```python
import functools

import jax
import jax.numpy as jnp
from jax import lax
from jax.experimental import pallas as pl
from jax.experimental.pallas import tpu as pltpu
from jax.sharding import PartitionSpec as P

F32, BF16 = jnp.float32, jnp.bfloat16
MESH = pl.DeviceIdType.MESH
CHANNELS, ROWS, COLS, LANES = 6, 16, 32, 128


def split_pair(value):
    high = value.astype(BF16)
    low = (value - high.astype(F32)).astype(BF16)
    return jnp.concatenate([high, low], axis=-1)


def flat(value):
    return value.reshape(-1, value.shape[-1])


def iota(shape, dim):
    return lax.broadcasted_iota(jnp.int32, shape, dim)


def self_product(value):
    pair = split_pair(value)
    return lax.dot_general(pair, pair, (((0,), (0,)), ((), ())), preferred_element_type=F32)


def gram_kernel(
    sizes, cells_total, fields,
    gram_out, north_out, south_out, west_out, east_out,
    body, last_raw, last, edge, north, south, west, east,
    pack_row, pack_col, pack_own, got_row, got_col,
    acc_one, acc_two, part, lat_buf, y_buf, z_buf, all_buf,
    load_sem, halo_send, halo_recv, lat_send, lat_recv, y_send, y_recv, z_send, z_recv, all_send, all_recv,
):
    n_lat, n_y, n_z = sizes
    n_lon = n_y * n_z
    lat, lon = lax.axis_index("lat"), lax.axis_index("lon")
    y, z = lon // n_z, lon % n_z
    above, below = lon - 1 + n_lon, lon + 1
    west_id, east_id = {"lon": above % n_lon}, {"lon": below % n_lon}

    def lat_peer(step):
        return (lat + step) % n_lat

    def y_peer(step):
        return (y + step) % n_y

    def z_peer(step):
        return (z + step) % n_z

    barrier = pltpu.get_barrier_semaphore()
    greeted = [west_id, east_id]
    greeted += [{"lat": lat_peer(step)} for step in range(1, n_lat)]
    greeted += [{"lon": y_peer(step) * n_z + z} for step in range(1, n_y)]
    greeted += [{"lon": y * n_z + z_peer(step)} for step in range(1, n_z)]
    for peer in greeted:
        pl.semaphore_signal(barrier, inc=1, device_id=peer, device_id_type=MESH)

    main = pl.ds(0, LANES)
    loads = [
        pltpu.make_async_copy(fields.at[:, :, :, main], body.at[:, pl.ds(0, ROWS), pl.ds(0, COLS), :], load_sem.at[0]),
        pltpu.make_async_copy(fields.at[:, :, :, pl.ds(LANES, 1)], last_raw, load_sem.at[1]),
        pltpu.make_async_copy(fields.at[:, :, COLS - 1, main], edge, load_sem.at[2]),
    ]
    for copy in loads:
        copy.start()

    body[:, ROWS : ROWS + 1, 0:COLS, :] = jnp.zeros((CHANNELS, 1, COLS, LANES), F32)
    body[:, :, COLS : COLS + 8, :] = jnp.zeros((CHANNELS, ROWS + 1, 8, LANES), F32)
    last[:, ROWS : ROWS + 1, 0:COLS, :] = jnp.zeros((CHANNELS, 1, COLS, LANES), F32)
    last[:, :, COLS : COLS + 8, :] = jnp.zeros((CHANNELS, ROWS + 1, 8, LANES), F32)
    acc_one[...] = jnp.zeros_like(acc_one)
    acc_two[...] = jnp.zeros_like(acc_two)

    loads[1].wait()
    for c in range(CHANNELS):
        last[c, 0:ROWS, 0:COLS, :] = jnp.broadcast_to(last_raw[c], (ROWS, COLS, LANES))

    lane8, sub8 = iota((8, LANES), 1), iota((8, LANES), 0)
    packed = jnp.zeros((8, LANES), F32)
    for c in range(CHANNELS):
        for t in range(COLS // 8):
            packed = jnp.where(lane8 == c * 4 + t, last[c, 0, 8 * t : 8 * t + 8, :], packed)
    pack_row[...] = packed

    def pack_column(j):
        packed = jnp.zeros((8, LANES), F32)
        for c in range(CHANNELS):
            for i in range(ROWS):
                one = jnp.broadcast_to(last[c, i, j : j + 1, :], (8, LANES))
                packed = jnp.where((lane8 == c * 2 + i // 8) & (sub8 == i % 8), one, packed)
        return packed

    pack_col[...] = pack_column(0)
    pack_own[...] = pack_column(COLS - 1)

    loads[0].wait()
    loads[2].wait()

    def sums(value, other):
        return (value * other).reshape(-1, 8, LANES).sum(axis=0)

    def plain(c, carry):
        cross, own = carry
        value = flat(body[c, 0:ROWS, 0:COLS, :])
        tail = flat(last[c, 0:ROWS, 0:COLS, :])
        acc_one[...] += self_product(value)
        return cross + sums(value, tail), own + sums(tail, tail)

    zero = jnp.zeros((8, LANES), F32)
    cross_one, own_one = lax.fori_loop(0, CHANNELS, plain, (zero, zero))

    pl.semaphore_wait(barrier, len(greeted))

    def remote(source, target, index, peer):
        return pltpu.make_async_remote_copy(
            source, target, halo_send.at[index], halo_recv.at[index], device_id=peer, device_id_type=MESH
        )

    lat_up = {"lat": lax.max(lat - 1, 0)}
    lat_down = {"lat": lax.min(lat + 1, n_lat - 1)}
    east_copies = [
        remote(fields.at[:, :, 0, main], east, 0, west_id),
        remote(pack_col, got_col, 1, west_id),
    ]
    south_copies = [
        remote(fields.at[:, 0, :, main], south, 2, lat_up),
        remote(pack_row, got_row, 3, lat_up),
    ]
    west_copy = remote(fields.at[:, :, COLS - 1, main], west, 4, east_id)
    north_copy = remote(fields.at[:, ROWS - 1, :, main], north, 5, lat_down)

    @pl.when(lat > 0)
    def _():
        for copy in south_copies:
            copy.start()

    for copy in east_copies:
        copy.start()

    @pl.when(lat < n_lat - 1)
    def _():
        north_copy.start()

    west_copy.start()

    def crossed(c, carry):
        cross, own = carry
        value = body[c, 0:ROWS, 0:COLS, :]
        tail = last[c, 0:ROWS, 0:COLS, :]
        lower = flat(value * body[c, 1 : ROWS + 1, 0:COLS, :])
        right = flat(value * body[c, 0:ROWS, 1 : COLS + 1, :])
        tail_lower = flat(tail * last[c, 1 : ROWS + 1, 0:COLS, :])
        tail_right = flat(tail * last[c, 0:ROWS, 1 : COLS + 1, :])
        acc_two[...] += self_product(lower)
        acc_two[...] += self_product(right)
        cross += sums(lower, tail_lower) + sums(right, tail_right)
        own += sums(tail_lower, tail_lower) + sums(tail_right, tail_right)
        return cross, own

    cross_two, own_two = lax.fori_loop(0, CHANNELS, crossed, (zero, zero))

    @pl.when(lat < n_lat - 1)
    def _():
        for copy in south_copies:
            copy.wait_recv()

    for copy in east_copies:
        copy.wait_recv()

    @pl.when(lat == n_lat - 1)
    def _():
        south[...] = jnp.zeros_like(south)
        got_row[...] = jnp.zeros_like(got_row)

    @pl.when(lat == 0)
    def _():
        north[...] = jnp.zeros_like(north)

    def spread(packed, lane):
        return jnp.broadcast_to(packed[:, lane : lane + 1], (8, LANES))

    row_packed, col_packed, own_packed = got_row[...], got_col[...], pack_own[...]
    tail_row = jnp.concatenate([spread(row_packed, lane) for lane in range(CHANNELS * 4)], axis=0)
    tail_row = tail_row * flat(last[:, ROWS - 1, 0:COLS, :])
    tail_col = [spread(col_packed, lane) * spread(own_packed, lane) for lane in range(CHANNELS * 2)]
    tails = jnp.concatenate([tail_row] + tail_col, axis=0)
    border = jnp.concatenate(
        [flat(body[:, ROWS - 1, 0:COLS, :] * south[...]), flat(edge[...] * east[...])], axis=0
    )
    acc_two[...] += self_product(border)
    cross_two += sums(border, tails)
    own_two += sums(tails, tails)

    total = acc_one[...] + 2.0 * acc_two[...]
    scale = 1.0 / cells_total
    full = (total[:LANES, :LANES] + total[LANES:, LANES:]) + (total[:LANES, LANES:] + total[LANES:, :LANES])
    full = full * scale
    cross = (cross_one + 2.0 * cross_two).sum(axis=0, keepdims=True) * scale
    own = (own_one + 2.0 * own_two).sum(axis=0, keepdims=True) * scale

    half = LANES // 2
    top, bottom = full[:half], full[half:]
    row, lane = iota((half, LANES), 0), iota((half, LANES), 1)
    folded = jnp.where((lane < half) & (row < lane), pltpu.roll(bottom, half, 1), top)
    diagonal = jnp.where(lane == row + half, bottom, 0.0).sum(axis=0, keepdims=True)
    extra = jnp.where(iota((1, LANES), 1) < half, own, diagonal)
    rows = half // n_lat
    for owner in range(n_lat):
        part[owner, 0:rows, :] = folded[owner * rows : (owner + 1) * rows]
        tail = cross if owner == 0 else extra if owner == 1 else jnp.zeros((1, LANES), F32)
        part[owner, rows : rows + 1, :] = tail

    def exchange(count, me, peer_of, device_of, source_of, buf, send, recv):
        copies = [
            pltpu.make_async_remote_copy(
                source_of(peer_of(step)), buf.at[me], send.at[step], recv.at[step],
                device_id=device_of(peer_of(step)), device_id_type=MESH,
            )
            for step in range(1, count)
        ]
        for copy in copies:
            copy.start()
        arrivals = [
            pltpu.make_async_remote_copy(
                buf.at[me], buf.at[peer_of(count - step)], send.at[step], recv.at[step],
                device_id=device_of(peer_of(step)), device_id_type=MESH,
            )
            for step in range(1, count)
        ]
        for copy in arrivals:
            copy.wait_recv()
        return copies

    def added(buf, count):
        result = buf[0]
        for index in range(1, count):
            result = result + buf[index]
        return result

    lat_buf[lat] = part[lat]
    pending = exchange(
        n_lat, lat, lat_peer, lambda p: {"lat": p}, lambda p: part.at[p], lat_buf, lat_send, lat_recv
    )
    y_buf[y] = added(lat_buf, n_lat)
    pending += exchange(
        n_y, y, y_peer, lambda p: {"lon": p * n_z + z}, lambda p: y_buf.at[y], y_buf, y_send, y_recv
    )
    z_buf[z] = added(y_buf, n_y)
    pending += exchange(
        n_z, z, z_peer, lambda p: {"lon": y * n_z + p}, lambda p: z_buf.at[z], z_buf, z_send, z_recv
    )
    all_buf[lat] = added(z_buf, n_z)
    pending += exchange(
        n_lat, lat, lat_peer, lambda p: {"lat": p}, lambda p: all_buf.at[lat], all_buf, all_send, all_recv
    )
    gram_out[...] = all_buf[...]

    @pl.when(lat > 0)
    def _():
        north_copy.wait_recv()
        for copy in south_copies:
            copy.wait_send()

    @pl.when(lat < n_lat - 1)
    def _():
        north_copy.wait_send()

    west_copy.wait_recv()
    for copy in [west_copy] + east_copies + pending:
        copy.wait_send()
    north_out[...] = north[...]
    south_out[...] = south[...]
    west_out[...] = west[...]
    east_out[...] = east[...]


def gram_call(fields, n_lat, n_lon):
    n_z = 8 if n_lon % 32 == 0 else max(n_lon // 2, 1)
    n_y = n_lon // n_z
    rows = LANES // 2 // n_lat + 1
    cells_total = 5 * CHANNELS * ROWS * n_lat * COLS * n_lon
    row_shape, col_shape = (CHANNELS, COLS, LANES), (CHANNELS, ROWS, LANES)
    chunk = (rows, LANES)
    dma = pltpu.SemaphoreType.DMA
    shapes = [(n_lat,) + chunk, row_shape, row_shape, col_shape, col_shape]
    vmem = pl.BlockSpec(memory_space=pltpu.VMEM)
    return pl.pallas_call(
        functools.partial(gram_kernel, (n_lat, n_y, n_z), cells_total),
        out_shape=[jax.ShapeDtypeStruct(shape, F32) for shape in shapes],
        in_specs=[pl.BlockSpec(memory_space=pl.ANY)],
        out_specs=[vmem] * 5,
        scratch_shapes=[
            pltpu.VMEM((CHANNELS, ROWS + 1, COLS + 8, LANES), F32),
            pltpu.VMEM((CHANNELS, ROWS, COLS, 1), F32),
            pltpu.VMEM((CHANNELS, ROWS + 1, COLS + 8, LANES), F32),
            pltpu.VMEM(col_shape, F32),
            pltpu.VMEM(row_shape, F32),
            pltpu.VMEM(row_shape, F32),
            pltpu.VMEM(col_shape, F32),
            pltpu.VMEM(col_shape, F32),
        ]
        + [pltpu.VMEM((8, LANES), F32)] * 5
        + [pltpu.VMEM((2 * LANES, 2 * LANES), F32)] * 2
        + [
            pltpu.VMEM((n_lat,) + chunk, F32),
            pltpu.VMEM((n_lat,) + chunk, F32),
            pltpu.VMEM((n_y,) + chunk, F32),
            pltpu.VMEM((n_z,) + chunk, F32),
            pltpu.VMEM((n_lat,) + chunk, F32),
            dma((3,)),
            dma((6,)), dma((6,)),
            dma((n_lat,)), dma((n_lat,)),
            dma((n_y,)), dma((n_y,)),
            dma((n_z,)), dma((n_z,)),
            dma((n_lat,)), dma((n_lat,)),
        ],
        compiler_params=pltpu.CompilerParams(
            collective_id=0, has_side_effects=True, vmem_limit_bytes=40 << 20
        ),
    )(fields)


def unfolded(gram):
    n_lat, rows, _ = gram.shape
    half = LANES // 2
    folded = jnp.concatenate([gram[owner, : rows - 1, :] for owner in range(n_lat)], axis=0)
    cross, extra = gram[0, rows - 1 : rows, :], gram[1, rows - 1 : rows, :]
    row, lane = iota((half, LANES), 0), iota((half, LANES), 1)
    top = jnp.where((lane < half) & (row <= lane), 0.0, folded)
    bottom = jnp.where((lane >= half) & (row < lane - half), pltpu.roll(folded, half, 1), 0.0)
    once = jnp.concatenate([top, bottom], axis=0)
    diagonal = jnp.concatenate(
        [jnp.where(lane == row, folded, 0.0), jnp.where(lane == row + half, jnp.broadcast_to(extra, (half, LANES)), 0.0)],
        axis=0,
    )
    full = once + once.T + diagonal
    row, lane = iota((LANES, LANES), 0), iota((LANES, LANES), 1)

    def column(line):
        return jnp.where(row == lane, jnp.broadcast_to(line, (LANES, LANES)), 0.0).sum(axis=1, keepdims=True)

    corner = extra[:, 0:1]
    shifted = pltpu.roll(pltpu.roll(full, LANES - 1, 0), LANES - 1, 1)
    line = jnp.where(iota((1, LANES), 1) == LANES - 1, corner, pltpu.roll(cross, LANES - 1, 1))
    shifted = jnp.where(lane == LANES - 1, column(line), shifted)
    shifted = jnp.where(row == LANES - 1, jnp.broadcast_to(line, (LANES, LANES)), shifted)
    identity = jnp.where(row == lane, 1.0, 0.0)
    first = jnp.where(lane == LANES - 1, column(cross), identity)
    low = jnp.where(row == LANES - 1, cross[:, 0:1], pltpu.roll(full, LANES - 1, 0)[:, 0:1])
    second = jnp.where(lane == LANES - 1, low, identity)
    return (full, first), (shifted, second)


def eliminate(b, work, c):
    start = pl.multiple_of(b * 8, 8)
    left = work[c, pl.ds(start, 8), 0:LANES]
    right = work[c, pl.ds(start, 8), LANES : 2 * LANES]
    block = pltpu.roll(left, (LANES - start) % LANES, 1)
    columns = [jnp.broadcast_to(block[:, j : j + 1], (8, LANES)) for j in range(8)]
    entry = {}
    for i in range(8):
        for j in range(i, 8):
            entry[i, j] = jnp.broadcast_to(columns[j][i : i + 1, :], (8, LANES))
    left_rows = [jnp.broadcast_to(left[i : i + 1, :], (8, LANES)) for i in range(8)]
    right_rows = [jnp.broadcast_to(right[i : i + 1, :], (8, LANES)) for i in range(8)]
    inverse = []
    for k in range(8):
        inverse.append(1.0 / entry[k, k])
        for i in range(k + 1, 8):
            factor = entry[k, i] * inverse[k]
            for j in range(i, 8):
                entry[i, j] = entry[i, j] - factor * entry[k, j]
            left_rows[i] = left_rows[i] - factor * left_rows[k]
            right_rows[i] = right_rows[i] - factor * right_rows[k]
    sub, lane = iota((8, LANES), 0), iota((8, LANES), 1)

    def gathered(rows):
        result = rows[0]
        for k in range(1, 8):
            result = jnp.where(sub == k, rows[k], result)
        return result

    pivots = gathered(inverse)
    done = gathered(left_rows)
    factors = jnp.where(lane >= start + 8, done * pivots, 0.0).T
    root = jnp.sqrt(pivots)
    work[c, pl.ds(start, 8), 0:LANES] = done * root
    work[c, pl.ds(start, 8), LANES : 2 * LANES] = gathered(right_rows) * root
    for t in range(16):
        rows = slice(8 * t, 8 * t + 8)
        lower_left = work[c, rows, 0:LANES]
        lower_right = work[c, rows, LANES : 2 * LANES]
        for k in range(8):
            factor = jnp.broadcast_to(factors[rows, k : k + 1], (8, LANES))
            lower_left = lower_left - factor * left_rows[k]
            lower_right = lower_right - factor * right_rows[k]
        work[c, rows, 0:LANES] = lower_left
        work[c, rows, LANES : 2 * LANES] = lower_right


def accurate(left, right):
    return lax.dot_general(
        left, right, (((1,), (1,)), ((), ())), precision=lax.Precision.HIGHEST, preferred_element_type=F32
    )


def modes_kernel(
    fields, gram, north, south, west, east, modes, forward, backward,
    body, work, weights, plain, lower, left, right, load_sem, store_sem,
):
    main = pl.ds(0, LANES)
    inner, across = pl.ds(1, ROWS), pl.ds(8, COLS)
    loads = [
        pltpu.make_async_copy(fields.at[:, :, :, main], body.at[:, inner, across, :], load_sem.at[0]),
        pltpu.make_async_copy(north, body.at[:, 0, across, :], load_sem.at[1]),
        pltpu.make_async_copy(south, body.at[:, ROWS + 1, across, :], load_sem.at[2]),
        pltpu.make_async_copy(west, body.at[:, inner, 7, :], load_sem.at[3]),
        pltpu.make_async_copy(east, body.at[:, inner, 8 + COLS, :], load_sem.at[4]),
    ]
    for copy in loads:
        copy.start()

    for c, (matrix, extended) in enumerate(unfolded(gram[...])):
        work[c, :, 0:LANES] = matrix
        work[c, :, LANES : 2 * LANES] = extended

    def step(b, carry):
        eliminate(b, work, 0)
        eliminate(b, work, 1)
        return carry

    lax.fori_loop(0, 16, step, 0)

    row, lane = iota((LANES, LANES), 0), iota((LANES, LANES), 1)

    def parts(c):
        factor, extended = work[c, :, 0:LANES], work[c, :, LANES : 2 * LANES]
        corner = jnp.where((row == LANES - 1) & (lane == LANES - 1), 1.0 / factor, 0.0)
        return factor, extended, jnp.where(lane == LANES - 1, corner, extended)

    factor, extended, inverse = parts(0)
    mixing = inverse.T
    high = mixing.astype(BF16)
    low = (mixing - high.astype(F32)).astype(BF16)
    line = jnp.concatenate([high, low], axis=1)
    weights[...] = jnp.concatenate([line, line], axis=0)

    for copy in loads:
        copy.wait()

    def mixed(value):
        both = jnp.dot(split_pair(value), weights[...], preferred_element_type=F32)
        return both[:, :LANES] + both[:, LANES:]

    def stores(c):
        return [
            pltpu.make_async_copy(plain.at[c], modes.at[c], store_sem.at[0, c]),
            pltpu.make_async_copy(lower.at[c, pl.ds(0, ROWS)], modes.at[CHANNELS + c], store_sem.at[1, c]),
            pltpu.make_async_copy(lower.at[c, pl.ds(1, ROWS)], modes.at[2 * CHANNELS + c], store_sem.at[2, c]),
            pltpu.make_async_copy(left.at[c], modes.at[3 * CHANNELS + c], store_sem.at[3, c]),
            pltpu.make_async_copy(right.at[c], modes.at[4 * CHANNELS + c], store_sem.at[4, c]),
        ]

    def channel(c, carry):
        value = body[c, 1 : ROWS + 1, 8 : 8 + COLS, :]
        shape = (ROWS, COLS, LANES)
        plain[c] = mixed(flat(value)).reshape(shape)
        pairs = body[c, 0 : ROWS + 1, 8 : 8 + COLS, :] * body[c, 1 : ROWS + 2, 8 : 8 + COLS, :]
        lower[c] = mixed(flat(pairs)).reshape((ROWS + 1, COLS, LANES))
        left[c] = mixed(flat(value * body[c, 1 : ROWS + 1, 7 : 7 + COLS, :])).reshape(shape)
        right[c] = mixed(flat(value * body[c, 1 : ROWS + 1, 9 : 9 + COLS, :])).reshape(shape)
        for copy in stores(c):
            copy.start()
        return carry

    lax.fori_loop(0, CHANNELS, channel, 0)

    shifted = jnp.where(lane == LANES - 1, extended, pltpu.roll(factor, LANES - 1, 1))
    forward[...] = accurate(shifted, inverse)
    factor, extended, inverse = parts(1)
    mixed_block = jnp.where(lane == 0, pltpu.roll(extended, 1, 1), pltpu.roll(factor, 1, 1))
    backward[...] = accurate(mixed_block, inverse)

    def finish(c, carry):
        for copy in stores(c):
            copy.wait()
        return carry

    lax.fori_loop(0, CHANNELS, finish, 0)


def modes_call(fields, gram, north, south, west, east):
    shape = (CHANNELS, ROWS, COLS, LANES)
    any_space = pl.BlockSpec(memory_space=pl.ANY)
    vmem = pl.BlockSpec(memory_space=pltpu.VMEM)
    return pl.pallas_call(
        modes_kernel,
        out_shape=[
            jax.ShapeDtypeStruct((5 * CHANNELS, ROWS, COLS, LANES), F32),
            jax.ShapeDtypeStruct((LANES, LANES), F32),
            jax.ShapeDtypeStruct((LANES, LANES), F32),
        ],
        in_specs=[any_space, vmem, any_space, any_space, any_space, any_space],
        out_specs=[any_space, vmem, vmem],
        scratch_shapes=[
            pltpu.VMEM((CHANNELS, ROWS + 2, COLS + 16, LANES), F32),
            pltpu.VMEM((2, LANES, 2 * LANES), F32),
            pltpu.VMEM((2 * LANES, 2 * LANES), BF16),
            pltpu.VMEM(shape, F32),
            pltpu.VMEM((CHANNELS, ROWS + 1, COLS, LANES), F32),
            pltpu.VMEM(shape, F32),
            pltpu.VMEM(shape, F32),
            pltpu.SemaphoreType.DMA((5,)),
            pltpu.SemaphoreType.DMA((5, CHANNELS)),
        ],
        compiler_params=pltpu.CompilerParams(vmem_limit_bytes=40 << 20),
    )(fields, gram, north, south, west, east)


def shards(fields):
    cells = fields.transpose(1, 2, 3, 0)
    gram, north, south, west, east = gram_call(cells, lax.axis_size("lat"), lax.axis_size("lon"))
    return tuple(modes_call(cells, gram, north, south, west, east))


def solution(mesh):
    return jax.shard_map(
        shards,
        mesh=mesh,
        in_specs=(P(None, None, "lat", "lon"),),
        out_specs=(P(None, "lat", "lon", None), P(), P()),
        check_vma=False,
    )
```

time: 395 us -> 57.7 us (0.15); the launches traced: 389 us -> 57.5 us
  waiting for transfers between devices: 239 us -> 0 us
  other arithmetic: 59.8 us -> 0 us
  Pallas kernels: 0 us -> 55 us
  matrix products: 40.3 us -> 0 us
  between operations: 16.9 us -> 0.65 us
  local copies, waits for them, and re-layouts: 17.8 us -> 1.88 us
  starting transfers between devices: 15.2 us -> 0 us
    psum x1 -> x0, waiting for transfers between devices: 239 us -> none  [shards(): gram_total = lax.psum(gram_local, ('lon', 'lat'))]
    another operation x11 -> x0, other arithmetic: 55.1 us -> none  [the longest x4 22.3 us: shards(): upper_factor = jnp.linalg.cholesky(gram_total).T]
    pallas_call x0 -> x2, Pallas kernels: none -> 55 us  [the longest x1 29.6 us: gram_call(): pl.pallas_call(functools.partial(gram_kernel, (n_lat, n_y, n_z), cells_to...]
    dot_general x5 -> x0, matrix products: 29.4 us -> none  [shards(): jnp.dot(flat_rows, flat_rows.T, precision=lax.Precision.HIGHEST)]
    ppermute x4 -> x0, starting transfers between devices: 15.1 us -> none  [the longest x2 11.1 us: with_halo(): lax.ppermute(lax.slice_in_dim(block, 0, width, axis=dim), axis, backward)]
    another operation x9 -> x0, matrix products: 10.9 us -> none  [the longest x5 8.3 us: shards(): jax.scipy.linalg.solve_triangular(head_block.T, flat_rows, lower=True)]
    slice x10 -> x0, local copies, waits for them, and re-layouts: 8.16 us -> none  [the longest x6 4.49 us: shards(): flat_rows = feature_slab.reshape(states, -1)[:snap_count]]
    unnamed x28 -> x2, local copies, waits for them, and re-layouts: 6.98 us -> 1.88 us
  transfers between devices with their start and end apart: 5 -> 0, of which waited for: 1 -> 0; matrix products, arithmetic and copies ran while one was open for 4% -> 0% of each run, Pallas kernels for 0% -> 0%
where the time goes in v1:
time: 57.7 us; the launch traced here: 57.5 us
  Pallas kernels  55 us (95%)
  local copies, waits for them, and re-layouts  1.88 us (3%)
  between operations  0.65 us (1%)
    pallas_call x1, Pallas kernels, gram_call(): pl.pallas_call(functools.partial(gram_kernel, (n_lat, n_y, n_z), cells_to...  29.6 us
    pallas_call x1, Pallas kernels, modes_call(): pl.pallas_call(modes_kernel, out_shape=[jax.ShapeDtypeStruct((5 * CHANNEL...  25.4 us
    unnamed x2, local copies, waits for them, and re-layouts  1.88 us

profile of v1, /device:TPU:1, one launch (start us, length us, event | category | flops | bytes accessed | tf_op | source)
XLA Modules:
  0.0 57.5 jit_solution(16165959473963911935)
XLA Ops:
  0.6 0.0 copy-start
  0.6 1.9 %copy-done = f32[129,6,16,32]{0,3,2,1:T(8,128)S(1)} copy-done((f32[129,6,16,32]{0,3,2,1:T(8,128)S(1)}, f32[129,6,16,32]{0,3,2,1:T(8,128)}, u32[]{:S(2)}) %copy-start) | copy-done | bytes 1585176
  2.5 29.6 %shard_map.38 = (f32[8,9,128]{2,1,0:T(8,128)S(1)}, f32[6,32,128]{2,1,0:T(8,128)S(1)}, f32[6,32,128]{2,1,0:T(8,128)S(1)}, f32[6,16,128]{2,1,0:T(8,128)S(1)}, f32[6,16,128]{2,1,0:T(8,128)S(1)}) custom-call(f32[6,16,32,129]{3,2,1,0:T(8,128)S(1)} %bitcast.1), custom_call_target="tpu_custom_call" | custom-call | tf_op jit(solution)/shard_map/pallas_call | solution.py:295
  32.1 25.4 %shard_map.39 = (f32[30,16,32,128]{3,2,1,0:T(8,128)}, f32[128,128]{1,0:T(8,128)}, f32[128,128]{1,0:T(8,128)}) custom-call(f32[6,16,32,129]{3,2,1,0:T(8,128)S(1)} %bitcast.2, f32[8,9,128]{2,1,0:T(8,128)S(1)} %get-tuple-element.8.gram, f32[6,32,128]{2,1,0:T(8,128)S(1)} %get-tuple-element.9.north, f32[6,32,128]{2,1,0:T(8,128)S(1)} %get-tuple-element.10.south, ...), custom_call_target="tpu_custom_call" | custom-call | tf_op jit(solution)/shard_map/pallas_call | solution.py:504
Async XLA Ops:
  0.6 1.9 %copy-start = (f32[129,6,16,32]{0,3,2,1:T(8,128)S(1)}, f32[129,6,16,32]{0,3,2,1:T(8,128)}, u32[]{:S(2)}) copy-start(f32[129,6,16,32]{0,3,2,1:T(8,128)} %param.1) | copy-start | bytes 4755460

commit v2 on v1

--- a/solution.py
+++ b/solution.py
@@ -359,18 +359,24 @@
     return (full, first), (shifted, second)
 
 
-def eliminate(b, work, c):
-    start = pl.multiple_of(b * 8, 8)
-    left = work[c, pl.ds(start, 8), 0:LANES]
-    right = work[c, pl.ds(start, 8), LANES : 2 * LANES]
-    block = pltpu.roll(left, (LANES - start) % LANES, 1)
-    columns = [jnp.broadcast_to(block[:, j : j + 1], (8, LANES)) for j in range(8)]
+def split_three(value):
+    one = value.astype(BF16).astype(F32)
+    two = (value - one).astype(BF16).astype(F32)
+    return one, two, value - one - two
+
+
+def eliminate(b, work, columns, first_row):
+    start = b * 8
+    sub, lane = iota((8, LANES), 0), iota((8, LANES), 1)
+    block = pltpu.roll(work[b, :, 0:LANES], (LANES - start) % LANES, 1)
+    for j in range(8):
+        columns[j] = jnp.broadcast_to(block[:, j : j + 1], (8, LANES))
     entry = {}
     for i in range(8):
         for j in range(i, 8):
-            entry[i, j] = jnp.broadcast_to(columns[j][i : i + 1, :], (8, LANES))
-    left_rows = [jnp.broadcast_to(left[i : i + 1, :], (8, LANES)) for i in range(8)]
-    right_rows = [jnp.broadcast_to(right[i : i + 1, :], (8, LANES)) for i in range(8)]
+            entry[i, j] = jnp.broadcast_to(columns[j, i : i + 1, :], (8, LANES))
+    left_rows = [jnp.broadcast_to(work[b, i : i + 1, 0:LANES], (8, LANES)) for i in range(8)]
+    right_rows = [jnp.broadcast_to(work[b, i : i + 1, LANES : 2 * LANES], (8, LANES)) for i in range(8)]
     inverse = []
     for k in range(8):
         inverse.append(1.0 / entry[k, k])
@@ -380,7 +386,6 @@
                 entry[i, j] = entry[i, j] - factor * entry[k, j]
             left_rows[i] = left_rows[i] - factor * left_rows[k]
             right_rows[i] = right_rows[i] - factor * right_rows[k]
-    sub, lane = iota((8, LANES), 0), iota((8, LANES), 1)
 
     def gathered(rows):
         result = rows[0]
@@ -389,21 +394,17 @@
         return result
 
     pivots = gathered(inverse)
-    done = gathered(left_rows)
-    factors = jnp.where(lane >= start + 8, done * pivots, 0.0).T
+    done_left, done_right = gathered(left_rows), gathered(right_rows)
+    f1, f2, f3 = split_three(jnp.where(lane >= start + 8, done_left * pivots, 0.0))
+    d1, d2, d3 = split_three(jnp.concatenate([done_left, done_right], axis=1))
+    factors = jnp.concatenate([f1, f1, f2, f1, f2, f3], axis=0).T.astype(BF16)
+    done = jnp.concatenate([d1, d2, d1, d3, d2, d1], axis=0).astype(BF16)
+    update = jnp.dot(factors[first_row:], done, preferred_element_type=F32)
     root = jnp.sqrt(pivots)
-    work[c, pl.ds(start, 8), 0:LANES] = done * root
-    work[c, pl.ds(start, 8), LANES : 2 * LANES] = gathered(right_rows) * root
-    for t in range(16):
-        rows = slice(8 * t, 8 * t + 8)
-        lower_left = work[c, rows, 0:LANES]
-        lower_right = work[c, rows, LANES : 2 * LANES]
-        for k in range(8):
-            factor = jnp.broadcast_to(factors[rows, k : k + 1], (8, LANES))
-            lower_left = lower_left - factor * left_rows[k]
-            lower_right = lower_right - factor * right_rows[k]
-        work[c, rows, 0:LANES] = lower_left
-        work[c, rows, LANES : 2 * LANES] = lower_right
+    work[b, :, 0:LANES] = done_left * root
+    work[b, :, LANES : 2 * LANES] = done_right * root
+    below = slice(first_row // 8, LANES // 8)
+    work[below] = work[below] - update.reshape(-1, 8, 2 * LANES)
 
 
 def accurate(left, right):
@@ -414,8 +415,9 @@
 
 def modes_kernel(
     fields, gram, north, south, west, east, modes, forward, backward,
-    body, work, weights, plain, lower, left, right, load_sem, store_sem,
+    body, work_one, work_two, splat_one, splat_two, weights, plain, lower, left, right, load_sem, store_sem,
 ):
+    works, splats = (work_one, work_two), (splat_one, splat_two)
     main = pl.ds(0, LANES)
     inner, across = pl.ds(1, ROWS), pl.ds(8, COLS)
     loads = [
@@ -428,21 +430,23 @@
     for copy in loads:
         copy.start()
 
-    for c, (matrix, extended) in enumerate(unfolded(gram[...])):
-        work[c, :, 0:LANES] = matrix
-        work[c, :, LANES : 2 * LANES] = extended
-
-    def step(b, carry):
-        eliminate(b, work, 0)
-        eliminate(b, work, 1)
-        return carry
-
-    lax.fori_loop(0, 16, step, 0)
+    for work, (matrix, extended) in zip(works, unfolded(gram[...])):
+        work[:, :, 0:LANES] = matrix.reshape(-1, 8, LANES)
+        work[:, :, LANES : 2 * LANES] = extended.reshape(-1, 8, LANES)
+
+    for phase in range(4):
+
+        def step(b, carry):
+            for work, columns in zip(works, splats):
+                eliminate(b, work, columns, phase * 32)
+            return carry
+
+        lax.fori_loop(phase * 4, phase * 4 + 4, step, 0)
 
     row, lane = iota((LANES, LANES), 0), iota((LANES, LANES), 1)
 
     def parts(c):
-        factor, extended = work[c, :, 0:LANES], work[c, :, LANES : 2 * LANES]
+        factor, extended = flat(works[c][:, :, 0:LANES]), flat(works[c][:, :, LANES : 2 * LANES])
         corner = jnp.where((row == LANES - 1) & (lane == LANES - 1), 1.0 / factor, 0.0)
         return factor, extended, jnp.where(lane == LANES - 1, corner, extended)
 
@@ -512,7 +516,10 @@
         out_specs=[any_space, vmem, vmem],
         scratch_shapes=[
             pltpu.VMEM((CHANNELS, ROWS + 2, COLS + 16, LANES), F32),
-            pltpu.VMEM((2, LANES, 2 * LANES), F32),
+            pltpu.VMEM((LANES // 8, 8, 2 * LANES), F32),
+            pltpu.VMEM((LANES // 8, 8, 2 * LANES), F32),
+            pltpu.VMEM((8, 8, LANES), F32),
+            pltpu.VMEM((8, 8, LANES), F32),
             pltpu.VMEM((2 * LANES, 2 * LANES), BF16),
             pltpu.VMEM(shape, F32),
             pltpu.VMEM((CHANNELS, ROWS + 1, COLS, LANES), F32),

time: 57.7 us -> 45.2 us (0.78)
  Pallas kernels: 55 us -> 42.5 us
    pallas_call x1, Pallas kernels: 25.4 us -> 12.9 us  [modes_call(): pl.pallas_call(modes_kernel, out_shape=[jax.ShapeDtypeStruct((5 * CHANNEL...]
where the time goes in v2:
time: 45.2 us; the launch traced here: 45.1 us
  Pallas kernels  42.5 us (94%)
  local copies, waits for them, and re-layouts  1.88 us (4%)
  between operations  0.65 us (1%)
    pallas_call x1, Pallas kernels, gram_call(): pl.pallas_call(functools.partial(gram_kernel, (n_lat, n_y, n_z), cells_to...  29.6 us
    pallas_call x1, Pallas kernels, modes_call(): pl.pallas_call(modes_kernel, out_shape=[jax.ShapeDtypeStruct((5 * CHANNEL...  12.9 us
    unnamed x2, local copies, waits for them, and re-layouts  1.88 us

profile of v2, /device:TPU:1, one launch (start us, length us, event | category | flops | bytes accessed | tf_op | source)
XLA Modules:
  0.0 45.1 jit_solution(10338031119276567659)
XLA Ops:
  0.6 0.0 copy-start
  0.6 1.9 %copy-done = f32[129,6,16,32]{0,3,2,1:T(8,128)S(1)} copy-done((f32[129,6,16,32]{0,3,2,1:T(8,128)S(1)}, f32[129,6,16,32]{0,3,2,1:T(8,128)}, u32[]{:S(2)}) %copy-start) | copy-done | bytes 1585176
  2.5 29.6 %shard_map.38 = (f32[8,9,128]{2,1,0:T(8,128)S(1)}, f32[6,32,128]{2,1,0:T(8,128)S(1)}, f32[6,32,128]{2,1,0:T(8,128)S(1)}, f32[6,16,128]{2,1,0:T(8,128)S(1)}, f32[6,16,128]{2,1,0:T(8,128)S(1)}) custom-call(f32[6,16,32,129]{3,2,1,0:T(8,128)S(1)} %bitcast.1), custom_call_target="tpu_custom_call" | custom-call | tf_op jit(solution)/shard_map/pallas_call | solution.py:295
  32.1 12.9 %shard_map.39 = (f32[30,16,32,128]{3,2,1,0:T(8,128)}, f32[128,128]{1,0:T(8,128)}, f32[128,128]{1,0:T(8,128)}) custom-call(f32[6,16,32,129]{3,2,1,0:T(8,128)S(1)} %bitcast.2, f32[8,9,128]{2,1,0:T(8,128)S(1)} %get-tuple-element.8.gram, f32[6,32,128]{2,1,0:T(8,128)S(1)} %get-tuple-element.9.north, f32[6,32,128]{2,1,0:T(8,128)S(1)} %get-tuple-element.10.south, ...), custom_call_target="tpu_custom_call" | custom-call | tf_op jit(solution)/shard_map/pallas_call | solution.py:508
Async XLA Ops:
  0.6 1.9 %copy-start = (f32[129,6,16,32]{0,3,2,1:T(8,128)S(1)}, f32[129,6,16,32]{0,3,2,1:T(8,128)}, u32[]{:S(2)}) copy-start(f32[129,6,16,32]{0,3,2,1:T(8,128)} %param.1) | copy-start | bytes 4755460

commit v3 on v2

--- a/solution.py
+++ b/solution.py
@@ -26,18 +26,27 @@
     return lax.broadcasted_iota(jnp.int32, shape, dim)
 
 
-def self_product(value):
-    pair = split_pair(value)
-    return lax.dot_general(pair, pair, (((0,), (0,)), ((), ())), preferred_element_type=F32)
+def sums(value, other):
+    return (value * other).reshape(-1, 8, LANES).sum(axis=0)
+
+
+def self_product(value, tails=None):
+    high = value.astype(BF16)
+    rest = value - high.astype(F32)
+    pair = jnp.concatenate([high, rest.astype(BF16)], axis=-1)
+    turned = high.T
+    if tails is not None:
+        turned = jnp.concatenate([turned, tails], axis=0)
+    return jnp.dot(turned, pair, preferred_element_type=F32), sums(rest, rest)
 
 
 def gram_kernel(
     sizes, cells_total, fields,
     gram_out, north_out, south_out, west_out, east_out,
-    body, last_raw, last, edge, north, south, west, east,
-    pack_row, pack_col, pack_own, got_row, got_col,
+    body, last, edge, north, south, west, east,
+    pack_row, pack_col, got_row, got_col, tail_cells, tails_ref,
     acc_one, acc_two, part, lat_buf, y_buf, z_buf, all_buf,
-    load_sem, halo_send, halo_recv, lat_send, lat_recv, y_send, y_recv, z_send, z_recv, all_send, all_recv,
+    load_sem, tail_sem, halo_send, halo_recv, lat_send, lat_recv, y_send, y_recv, z_send, z_recv, all_send, all_recv,
 ):
     n_lat, n_y, n_z = sizes
     n_lon = n_y * n_z
@@ -64,61 +73,26 @@
         pl.semaphore_signal(barrier, inc=1, device_id=peer, device_id_type=MESH)
 
     main = pl.ds(0, LANES)
-    loads = [
-        pltpu.make_async_copy(fields.at[:, :, :, main], body.at[:, pl.ds(0, ROWS), pl.ds(0, COLS), :], load_sem.at[0]),
-        pltpu.make_async_copy(fields.at[:, :, :, pl.ds(LANES, 1)], last_raw, load_sem.at[1]),
-        pltpu.make_async_copy(fields.at[:, :, COLS - 1, main], edge, load_sem.at[2]),
-    ]
-    for copy in loads:
-        copy.start()
-
-    body[:, ROWS : ROWS + 1, 0:COLS, :] = jnp.zeros((CHANNELS, 1, COLS, LANES), F32)
-    body[:, :, COLS : COLS + 8, :] = jnp.zeros((CHANNELS, ROWS + 1, 8, LANES), F32)
-    last[:, ROWS : ROWS + 1, 0:COLS, :] = jnp.zeros((CHANNELS, 1, COLS, LANES), F32)
-    last[:, :, COLS : COLS + 8, :] = jnp.zeros((CHANNELS, ROWS + 1, 8, LANES), F32)
-    acc_one[...] = jnp.zeros_like(acc_one)
-    acc_two[...] = jnp.zeros_like(acc_two)
-
-    loads[1].wait()
-    for c in range(CHANNELS):
-        last[c, 0:ROWS, 0:COLS, :] = jnp.broadcast_to(last_raw[c], (ROWS, COLS, LANES))
-
-    lane8, sub8 = iota((8, LANES), 1), iota((8, LANES), 0)
-    packed = jnp.zeros((8, LANES), F32)
-    for c in range(CHANNELS):
-        for t in range(COLS // 8):
-            packed = jnp.where(lane8 == c * 4 + t, last[c, 0, 8 * t : 8 * t + 8, :], packed)
-    pack_row[...] = packed
-
-    def pack_column(j):
-        packed = jnp.zeros((8, LANES), F32)
-        for c in range(CHANNELS):
-            for i in range(ROWS):
-                one = jnp.broadcast_to(last[c, i, j : j + 1, :], (8, LANES))
-                packed = jnp.where((lane8 == c * 2 + i // 8) & (sub8 == i % 8), one, packed)
-        return packed
-
-    pack_col[...] = pack_column(0)
-    pack_own[...] = pack_column(COLS - 1)
-
-    loads[0].wait()
-    loads[2].wait()
-
-    def sums(value, other):
-        return (value * other).reshape(-1, 8, LANES).sum(axis=0)
-
-    def plain(c, carry):
-        cross, own = carry
-        value = flat(body[c, 0:ROWS, 0:COLS, :])
-        tail = flat(last[c, 0:ROWS, 0:COLS, :])
-        acc_one[...] += self_product(value)
-        return cross + sums(value, tail), own + sums(tail, tail)
-
-    zero = jnp.zeros((8, LANES), F32)
-    cross_one, own_one = lax.fori_loop(0, CHANNELS, plain, (zero, zero))
+
+    def load(c):
+        return pltpu.make_async_copy(
+            fields.at[c, :, :, main], body.at[c, pl.ds(0, ROWS), pl.ds(0, COLS), :], load_sem.at[c]
+        )
+
+    tail_load = pltpu.make_async_copy(
+        fields.at[:, :, :, pl.ds(LANES, 1)], last, tail_sem.at[0]
+    )
+    edge_load = pltpu.make_async_copy(fields.at[:, :, COLS - 1, main], edge, tail_sem.at[1])
+    tail_load.start()
+
+    def start_load(c, carry):
+        load(c).start()
+        return carry
+
+    lax.fori_loop(0, CHANNELS, start_load, 0)
+    edge_load.start()
 
     pl.semaphore_wait(barrier, len(greeted))
-
     def remote(source, target, index, peer):
         return pltpu.make_async_remote_copy(
             source, target, halo_send.at[index], halo_recv.at[index], device_id=peer, device_id_type=MESH
@@ -139,11 +113,9 @@
 
     @pl.when(lat > 0)
     def _():
-        for copy in south_copies:
-            copy.start()
-
-    for copy in east_copies:
-        copy.start()
+        south_copies[0].start()
+
+    east_copies[0].start()
 
     @pl.when(lat < n_lat - 1)
     def _():
@@ -151,21 +123,77 @@
 
     west_copy.start()
 
-    def crossed(c, carry):
-        cross, own = carry
+    body[:, ROWS : ROWS + 1, 0:COLS, :] = jnp.zeros((CHANNELS, 1, COLS, LANES), F32)
+    body[:, :, COLS : COLS + 8, :] = jnp.zeros((CHANNELS, ROWS + 1, 8, LANES), F32)
+    acc_one[...] = jnp.zeros_like(acc_one)
+    acc_two[...] = jnp.zeros_like(acc_two)
+
+    tail_load.wait()
+    wide_lane = iota((LANES, LANES), 1)
+    merged = jnp.zeros((LANES, LANES), F32)
+    for c in range(CHANNELS):
+        for q in range(4):
+            line = last[c, 4 * q : 4 * q + 4].reshape(LANES, 1)
+            merged = jnp.where(wide_lane == 4 * c + q, jnp.broadcast_to(line, (LANES, LANES)), merged)
+    tail_cells[...] = merged
+    pack_row[...] = merged[0:COLS]
+    sub8 = iota((8, LANES), 0)
+
+    def column(ref_or_value, j):
+        lines = [jnp.broadcast_to(ref_or_value[COLS * i + j : COLS * i + j + 1, :], (8, LANES)) for i in range(4)]
+        result = lines[3]
+        for i in range(3):
+            result = jnp.where(sub8 == i, lines[i], result)
+        return result
+
+    pack_col[...] = column(tail_cells, 0)
+    east_copies[1].start()
+
+    @pl.when(lat > 0)
+    def _():
+        south_copies[1].start()
+
+    count = 4 * CHANNELS
+    tail = merged.T[:count]
+    row, lane = iota((count, LANES), 0), iota((count, LANES), 1)
+    right = tail * jnp.where(lane % COLS == COLS - 1, 0.0, pltpu.roll(tail, LANES - 1, 1))
+    ahead = pltpu.roll(tail, LANES - COLS, 1)
+    further = jnp.where(row % 4 == 3, 0.0, pltpu.roll(ahead, count - 1, 0))
+    lower = tail * jnp.where(lane < LANES - COLS, ahead, further)
+    for f, values in enumerate((tail, lower, right)):
+        high = values.astype(BF16).astype(F32)
+        low = values - high
+        for pair in range(CHANNELS // 2):
+            high8, low8 = high[8 * pair : 8 * pair + 8], low[8 * pair : 8 * pair + 8]
+            first = jnp.where(sub8 < 4, high8, pltpu.roll(low8, 4, 0))
+            second = jnp.where(sub8 < 4, pltpu.roll(high8, 4, 0), low8)
+            for c, both in ((2 * pair, first), (2 * pair + 1, second)):
+                for q in range(4):
+                    part_q = jnp.where(sub8 % 4 == q, both, 0.0)
+                    part_q = jnp.concatenate([part_q, jnp.zeros((8, LANES), F32)], axis=0)
+                    tails_ref[f, c, :, LANES * q : LANES * q + LANES] = part_q.astype(BF16)
+    own_one = sums(tail, tail)
+    own_two = sums(lower, lower) + sums(right, right)
+
+    zero = jnp.zeros((8, LANES), F32)
+
+    def channel(c, carry):
+        rest_one, rest_two = carry
+        load(c).wait()
         value = body[c, 0:ROWS, 0:COLS, :]
-        tail = last[c, 0:ROWS, 0:COLS, :]
-        lower = flat(value * body[c, 1 : ROWS + 1, 0:COLS, :])
-        right = flat(value * body[c, 0:ROWS, 1 : COLS + 1, :])
-        tail_lower = flat(tail * last[c, 1 : ROWS + 1, 0:COLS, :])
-        tail_right = flat(tail * last[c, 0:ROWS, 1 : COLS + 1, :])
-        acc_two[...] += self_product(lower)
-        acc_two[...] += self_product(right)
-        cross += sums(lower, tail_lower) + sums(right, tail_right)
-        own += sums(tail_lower, tail_lower) + sums(tail_right, tail_right)
-        return cross, own
-
-    cross_two, own_two = lax.fori_loop(0, CHANNELS, crossed, (zero, zero))
+        product, rest = self_product(flat(value), tails_ref[0, c])
+        acc_one[...] += product
+        rest_one += rest
+        product, rest = self_product(flat(value * body[c, 1 : ROWS + 1, 0:COLS, :]), tails_ref[1, c])
+        acc_two[...] += product
+        rest_two += rest
+        product, rest = self_product(flat(value * body[c, 0:ROWS, 1 : COLS + 1, :]), tails_ref[2, c])
+        acc_two[...] += product
+        rest_two += rest
+        return rest_one, rest_two
+
+    rest_one, rest_two = lax.fori_loop(0, CHANNELS, channel, (zero, zero))
+    edge_load.wait()
 
     @pl.when(lat < n_lat - 1)
     def _():
@@ -187,24 +215,35 @@
     def spread(packed, lane):
         return jnp.broadcast_to(packed[:, lane : lane + 1], (8, LANES))
 
-    row_packed, col_packed, own_packed = got_row[...], got_col[...], pack_own[...]
-    tail_row = jnp.concatenate([spread(row_packed, lane) for lane in range(CHANNELS * 4)], axis=0)
-    tail_row = tail_row * flat(last[:, ROWS - 1, 0:COLS, :])
-    tail_col = [spread(col_packed, lane) * spread(own_packed, lane) for lane in range(CHANNELS * 2)]
-    tails = jnp.concatenate([tail_row] + tail_col, axis=0)
+    row_pairs = pltpu.roll(tail_cells[LANES - COLS : LANES, :], LANES - 3, 1) * got_row[...]
+    column_pairs = column(tail_cells, COLS - 1) * got_col[...]
+    column_pairs = jnp.where(sub8 < 4, column_pairs, pltpu.roll(pltpu.roll(column_pairs, 4, 0), LANES - 1, 1))
+    tails = [
+        spread(row_pairs[8 * t : 8 * t + 8], 4 * c) for c in range(CHANNELS) for t in range(COLS // 8)
+    ]
+    tails += [spread(column_pairs, 4 * c + 2 * h) for c in range(CHANNELS) for h in range(2)]
+    tails = jnp.concatenate(tails, axis=0)
     border = jnp.concatenate(
         [flat(body[:, ROWS - 1, 0:COLS, :] * south[...]), flat(edge[...] * east[...])], axis=0
     )
-    acc_two[...] += self_product(border)
-    cross_two += sums(border, tails)
-    own_two += sums(tails, tails)
-
-    total = acc_one[...] + 2.0 * acc_two[...]
+    product, rest = self_product(border)
+    rest_two += rest
+    cross_two = sums(border, tails)
+    border_own = sums(tails, tails).sum(axis=0, keepdims=True)
+
     scale = 1.0 / cells_total
-    full = (total[:LANES, :LANES] + total[LANES:, LANES:]) + (total[:LANES, LANES:] + total[LANES:, :LANES])
-    full = full * scale
-    cross = (cross_one + 2.0 * cross_two).sum(axis=0, keepdims=True) * scale
-    own = (own_one + 2.0 * own_two).sum(axis=0, keepdims=True) * scale
+    total = (acc_one[...] + 2.0 * acc_two[...]) * scale
+    rest = (rest_one + 2.0 * rest_two).sum(axis=0, keepdims=True) * scale
+    square = total[:LANES] + product * (2.0 * scale)
+    twisted = square[:, LANES:]
+    full = square[:, :LANES] + (twisted + twisted.T)
+    full += jnp.where(iota((LANES, LANES), 0) == iota((LANES, LANES), 1), rest, 0.0)
+    cross = cross_two.sum(axis=0, keepdims=True) * (2.0 * scale)
+    mixed = total[LANES : LANES + 8]
+    mixed = mixed[:, :LANES] + jnp.where(sub8 < 4, mixed[:, LANES:], 0.0)
+    cross += mixed.sum(axis=0, keepdims=True)
+    own = (own_one + 2.0 * own_two).sum(axis=0, keepdims=True).sum(axis=1, keepdims=True)
+    own = (jnp.broadcast_to(own, (1, LANES)) + 2.0 * border_own) * scale
 
     half = LANES // 2
     top, bottom = full[:half], full[half:]
@@ -219,25 +258,17 @@
         part[owner, rows : rows + 1, :] = tail
 
     def exchange(count, me, peer_of, device_of, source_of, buf, send, recv):
-        copies = [
+        def start(step, carry):
+            peer = peer_of(step)
             pltpu.make_async_remote_copy(
-                source_of(peer_of(step)), buf.at[me], send.at[step], recv.at[step],
-                device_id=device_of(peer_of(step)), device_id_type=MESH,
-            )
-            for step in range(1, count)
-        ]
-        for copy in copies:
-            copy.start()
-        arrivals = [
-            pltpu.make_async_remote_copy(
-                buf.at[me], buf.at[peer_of(count - step)], send.at[step], recv.at[step],
-                device_id=device_of(peer_of(step)), device_id_type=MESH,
-            )
-            for step in range(1, count)
-        ]
-        for copy in arrivals:
-            copy.wait_recv()
-        return copies
+                source_of(peer), buf.at[me], send.at[0], recv.at[0], device_id=device_of(peer), device_id_type=MESH
+            ).start()
+            return carry
+
+        lax.fori_loop(1, count, start, 0)
+        others = buf.at[pl.ds(0, count - 1)]
+        pltpu.make_async_copy(others, others, recv.at[0]).wait()
+        return pltpu.make_async_copy(others, others, send.at[0])
 
     def added(buf, count):
         result = buf[0]
@@ -246,21 +277,21 @@
         return result
 
     lat_buf[lat] = part[lat]
-    pending = exchange(
+    pending = [exchange(
         n_lat, lat, lat_peer, lambda p: {"lat": p}, lambda p: part.at[p], lat_buf, lat_send, lat_recv
-    )
+    )]
     y_buf[y] = added(lat_buf, n_lat)
-    pending += exchange(
+    pending += [exchange(
         n_y, y, y_peer, lambda p: {"lon": p * n_z + z}, lambda p: y_buf.at[y], y_buf, y_send, y_recv
-    )
+    )]
     z_buf[z] = added(y_buf, n_y)
-    pending += exchange(
+    pending += [exchange(
         n_z, z, z_peer, lambda p: {"lon": y * n_z + p}, lambda p: z_buf.at[z], z_buf, z_send, z_recv
-    )
+    )]
     all_buf[lat] = added(z_buf, n_z)
-    pending += exchange(
+    pending += [exchange(
         n_lat, lat, lat_peer, lambda p: {"lat": p}, lambda p: all_buf.at[lat], all_buf, all_send, all_recv
-    )
+    )]
     gram_out[...] = all_buf[...]
 
     @pl.when(lat > 0)
@@ -274,8 +305,10 @@
         north_copy.wait_send()
 
     west_copy.wait_recv()
-    for copy in [west_copy] + east_copies + pending:
+    for copy in [west_copy] + east_copies:
         copy.wait_send()
+    for copy in pending:
+        copy.wait()
     north_out[...] = north[...]
     south_out[...] = south[...]
     west_out[...] = west[...]
@@ -295,35 +328,35 @@
     return pl.pallas_call(
         functools.partial(gram_kernel, (n_lat, n_y, n_z), cells_total),
         out_shape=[jax.ShapeDtypeStruct(shape, F32) for shape in shapes],
-        in_specs=[pl.BlockSpec(memory_space=pl.ANY)],
+        in_specs=[pl.BlockSpec(memory_space=pltpu.HBM)],
         out_specs=[vmem] * 5,
         scratch_shapes=[
             pltpu.VMEM((CHANNELS, ROWS + 1, COLS + 8, LANES), F32),
             pltpu.VMEM((CHANNELS, ROWS, COLS, 1), F32),
-            pltpu.VMEM((CHANNELS, ROWS + 1, COLS + 8, LANES), F32),
             pltpu.VMEM(col_shape, F32),
             pltpu.VMEM(row_shape, F32),
             pltpu.VMEM(row_shape, F32),
             pltpu.VMEM(col_shape, F32),
             pltpu.VMEM(col_shape, F32),
         ]
-        + [pltpu.VMEM((8, LANES), F32)] * 5
-        + [pltpu.VMEM((2 * LANES, 2 * LANES), F32)] * 2
+        + [pltpu.VMEM((COLS, LANES), F32), pltpu.VMEM((8, LANES), F32)] * 2
+        + [pltpu.VMEM((LANES, LANES), F32), pltpu.VMEM((3, CHANNELS, 16, 4 * LANES), BF16)]
+        + [pltpu.VMEM((LANES + 16, 2 * LANES), F32)] * 2
         + [
             pltpu.VMEM((n_lat,) + chunk, F32),
             pltpu.VMEM((n_lat,) + chunk, F32),
             pltpu.VMEM((n_y,) + chunk, F32),
             pltpu.VMEM((n_z,) + chunk, F32),
             pltpu.VMEM((n_lat,) + chunk, F32),
-            dma((3,)),
+            dma((CHANNELS,)), dma((2,)),
             dma((6,)), dma((6,)),
-            dma((n_lat,)), dma((n_lat,)),
-            dma((n_y,)), dma((n_y,)),
-            dma((n_z,)), dma((n_z,)),
-            dma((n_lat,)), dma((n_lat,)),
+            dma((1,)), dma((1,)),
+            dma((1,)), dma((1,)),
+            dma((1,)), dma((1,)),
+            dma((1,)), dma((1,)),
         ],
         compiler_params=pltpu.CompilerParams(
-            collective_id=0, has_side_effects=True, vmem_limit_bytes=40 << 20
+            collective_id=0, has_side_effects=True, vmem_limit_bytes=64_500_000
         ),
     )(fields)
 
@@ -512,7 +545,7 @@
             jax.ShapeDtypeStruct((LANES, LANES), F32),
             jax.ShapeDtypeStruct((LANES, LANES), F32),
         ],
-        in_specs=[any_space, vmem, any_space, any_space, any_space, any_space],
+        in_specs=[pl.BlockSpec(memory_space=pltpu.HBM), vmem, any_space, any_space, any_space, any_space],
         out_specs=[any_space, vmem, vmem],
         scratch_shapes=[
             pltpu.VMEM((CHANNELS, ROWS + 2, COLS + 16, LANES), F32),
@@ -528,7 +561,7 @@
             pltpu.SemaphoreType.DMA((5,)),
             pltpu.SemaphoreType.DMA((5, CHANNELS)),
         ],
-        compiler_params=pltpu.CompilerParams(vmem_limit_bytes=40 << 20),
+        compiler_params=pltpu.CompilerParams(vmem_limit_bytes=64_500_000),
     )(fields, gram, north, south, west, east)
 
 

time: 45.2 us -> 44.8 us (level)
  local copies, waits for them, and re-layouts: 1.88 us -> 0 us
  Pallas kernels: 42.5 us -> 44 us
    unnamed x2 -> x0, local copies, waits for them, and re-layouts: 1.88 us -> none
    pallas_call x1, Pallas kernels: 29.6 us -> 30.4 us  [gram_call(): pl.pallas_call(functools.partial(gram_kernel, (n_lat, n_y, n_z), cells_to...]
    pallas_call x1, Pallas kernels: 12.9 us -> 13.6 us  [modes_call(): pl.pallas_call(modes_kernel, out_shape=[jax.ShapeDtypeStruct((5 * CHANNEL...]
where the time goes in v3:
time: 44.8 us; the launch traced here: 44.6 us
  Pallas kernels  44 us (98%)
  between operations  0.64 us (1%)
    pallas_call x1, Pallas kernels, gram_call(): pl.pallas_call(functools.partial(gram_kernel, (n_lat, n_y, n_z), cells_to...  30.4 us
    pallas_call x1, Pallas kernels, modes_call(): pl.pallas_call(modes_kernel, out_shape=[jax.ShapeDtypeStruct((5 * CHANNEL...  13.6 us

profile of v3, /device:TPU:1, one launch (start us, length us, event | category | flops | bytes accessed | tf_op | source)
XLA Modules:
  0.0 44.6 jit_solution(5852862647318667001)
XLA Ops:
  0.6 30.4 %shard_map.38 = (f32[8,9,128]{2,1,0:T(8,128)}, f32[6,32,128]{2,1,0:T(8,128)}, f32[6,32,128]{2,1,0:T(8,128)}, f32[6,16,128]{2,1,0:T(8,128)}, f32[6,16,128]{2,1,0:T(8,128)}) custom-call(f32[6,16,32,129]{3,2,1,0:T(8,128)} %bitcast.1), custom_call_target="tpu_custom_call" | custom-call | tf_op jit(solution)/shard_map/pallas_call | solution.py:328
  31.0 13.6 %shard_map.39 = (f32[30,16,32,128]{3,2,1,0:T(8,128)}, f32[128,128]{1,0:T(8,128)}, f32[128,128]{1,0:T(8,128)}) custom-call(f32[6,16,32,129]{3,2,1,0:T(8,128)} %bitcast.2, f32[8,9,128]{2,1,0:T(8,128)} %get-tuple-element.8.gram, f32[6,32,128]{2,1,0:T(8,128)} %get-tuple-element.9.north, f32[6,32,128]{2,1,0:T(8,128)} %get-tuple-element.10.south, ...), custom_call_target="tpu_custom_call" | custom-call | tf_op jit(solution)/shard_map/pallas_call | solution.py:541

commit v4 on v3

--- a/solution.py
+++ b/solution.py
@@ -192,7 +192,7 @@
         rest_two += rest
         return rest_one, rest_two
 
-    rest_one, rest_two = lax.fori_loop(0, CHANNELS, channel, (zero, zero))
+    rest_one, rest_two = lax.fori_loop(0, CHANNELS, channel, (zero, zero), unroll=True)
     edge_load.wait()
 
     @pl.when(lat < n_lat - 1)
@@ -356,7 +356,7 @@
             dma((1,)), dma((1,)),
         ],
         compiler_params=pltpu.CompilerParams(
-            collective_id=0, has_side_effects=True, vmem_limit_bytes=64_500_000
+            collective_id=0, has_side_effects=True, vmem_limit_bytes=48 << 20
         ),
     )(fields)
 
@@ -398,18 +398,24 @@
     return one, two, value - one - two
 
 
-def eliminate(b, work, columns, first_row):
+def eliminate(b, works, splats, first_row):
     start = b * 8
     sub, lane = iota((8, LANES), 0), iota((8, LANES), 1)
-    block = pltpu.roll(work[b, :, 0:LANES], (LANES - start) % LANES, 1)
-    for j in range(8):
-        columns[j] = jnp.broadcast_to(block[:, j : j + 1], (8, LANES))
+    upper = sub < 4
+    for work, columns in zip(works, splats):
+        block = pltpu.roll(work[b, :, 0:LANES], (LANES - start) % LANES, 1)
+        for j in range(8):
+            columns[j] = jnp.broadcast_to(block[:, j : j + 1], (8, LANES))
+
+    def paired(first, second):
+        return jnp.where(upper, jnp.broadcast_to(first, (8, LANES)), jnp.broadcast_to(second, (8, LANES)))
+
     entry = {}
     for i in range(8):
         for j in range(i, 8):
-            entry[i, j] = jnp.broadcast_to(columns[j, i : i + 1, :], (8, LANES))
-    left_rows = [jnp.broadcast_to(work[b, i : i + 1, 0:LANES], (8, LANES)) for i in range(8)]
-    right_rows = [jnp.broadcast_to(work[b, i : i + 1, LANES : 2 * LANES], (8, LANES)) for i in range(8)]
+            entry[i, j] = paired(*[columns[j, i : i + 1, :] for columns in splats])
+    left_rows = [paired(*[work[b, i : i + 1, 0:LANES] for work in works]) for i in range(8)]
+    right_rows = [paired(*[work[b, i : i + 1, LANES : 2 * LANES] for work in works]) for i in range(8)]
     inverse = []
     for k in range(8):
         inverse.append(1.0 / entry[k, k])
@@ -421,23 +427,25 @@
             right_rows[i] = right_rows[i] - factor * right_rows[k]
 
     def gathered(rows):
-        result = rows[0]
-        for k in range(1, 8):
-            result = jnp.where(sub == k, rows[k], result)
-        return result
-
-    pivots = gathered(inverse)
-    done_left, done_right = gathered(left_rows), gathered(right_rows)
-    f1, f2, f3 = split_three(jnp.where(lane >= start + 8, done_left * pivots, 0.0))
-    d1, d2, d3 = split_three(jnp.concatenate([done_left, done_right], axis=1))
-    factors = jnp.concatenate([f1, f1, f2, f1, f2, f3], axis=0).T.astype(BF16)
-    done = jnp.concatenate([d1, d2, d1, d3, d2, d1], axis=0).astype(BF16)
-    update = jnp.dot(factors[first_row:], done, preferred_element_type=F32)
-    root = jnp.sqrt(pivots)
-    work[b, :, 0:LANES] = done_left * root
-    work[b, :, LANES : 2 * LANES] = done_right * root
+        low, high = rows[0], rows[4]
+        for k in range(1, 4):
+            low = jnp.where(sub % 4 == k, rows[k], low)
+            high = jnp.where(sub % 4 == k, rows[4 + k], high)
+        return jnp.where(upper, low, pltpu.roll(high, 4, 0)), jnp.where(upper, pltpu.roll(low, 4, 0), high)
+
     below = slice(first_row // 8, LANES // 8)
-    work[below] = work[below] - update.reshape(-1, 8, 2 * LANES)
+    for work, pivots, done_left, done_right in zip(
+        works, gathered(inverse), gathered(left_rows), gathered(right_rows)
+    ):
+        f1, f2, f3 = split_three(jnp.where(lane >= start + 8, done_left * pivots, 0.0))
+        d1, d2, d3 = split_three(jnp.concatenate([done_left, done_right], axis=1))
+        factors = jnp.concatenate([f1, f1, f2, f1, f2, f3], axis=0).T.astype(BF16)
+        done = jnp.concatenate([d1, d2, d1, d3, d2, d1], axis=0).astype(BF16)
+        update = jnp.dot(factors[first_row:], done, preferred_element_type=F32)
+        root = jnp.sqrt(pivots)
+        work[b, :, 0:LANES] = done_left * root
+        work[b, :, LANES : 2 * LANES] = done_right * root
+        work[below] = work[below] - update.reshape(-1, 8, 2 * LANES)
 
 
 def accurate(left, right):
@@ -448,17 +456,18 @@
 
 def modes_kernel(
     fields, gram, north, south, west, east, modes, forward, backward,
-    body, work_one, work_two, splat_one, splat_two, weights, plain, lower, left, right, load_sem, store_sem,
+    body, work_one, work_two, splat_one, splat_two, weights, first_column, plain, lower, left, right,
+    load_sem, store_sem,
 ):
     works, splats = (work_one, work_two), (splat_one, splat_two)
     main = pl.ds(0, LANES)
-    inner, across = pl.ds(1, ROWS), pl.ds(8, COLS)
+    inner = pl.ds(1, ROWS)
     loads = [
-        pltpu.make_async_copy(fields.at[:, :, :, main], body.at[:, inner, across, :], load_sem.at[0]),
-        pltpu.make_async_copy(north, body.at[:, 0, across, :], load_sem.at[1]),
-        pltpu.make_async_copy(south, body.at[:, ROWS + 1, across, :], load_sem.at[2]),
-        pltpu.make_async_copy(west, body.at[:, inner, 7, :], load_sem.at[3]),
-        pltpu.make_async_copy(east, body.at[:, inner, 8 + COLS, :], load_sem.at[4]),
+        pltpu.make_async_copy(fields.at[:, :, :, main], body.at[:, inner, pl.ds(0, COLS), :], load_sem.at[0]),
+        pltpu.make_async_copy(north, body.at[:, 0, pl.ds(0, COLS), :], load_sem.at[1]),
+        pltpu.make_async_copy(south, body.at[:, ROWS + 1, pl.ds(0, COLS), :], load_sem.at[2]),
+        pltpu.make_async_copy(fields.at[:, :, 0, main], first_column, load_sem.at[3]),
+        pltpu.make_async_copy(east, body.at[:, inner, COLS, :], load_sem.at[4]),
     ]
     for copy in loads:
         copy.start()
@@ -470,8 +479,7 @@
     for phase in range(4):
 
         def step(b, carry):
-            for work, columns in zip(works, splats):
-                eliminate(b, work, columns, phase * 32)
+            eliminate(b, works, splats, phase * 32)
             return carry
 
         lax.fori_loop(phase * 4, phase * 4 + 4, step, 0)
@@ -497,28 +505,39 @@
         both = jnp.dot(split_pair(value), weights[...], preferred_element_type=F32)
         return both[:, :LANES] + both[:, LANES:]
 
+    inner_cols, outer_cols = pl.ds(0, COLS - 1), pl.ds(1, COLS - 1)
+
     def stores(c):
         return [
             pltpu.make_async_copy(plain.at[c], modes.at[c], store_sem.at[0, c]),
             pltpu.make_async_copy(lower.at[c, pl.ds(0, ROWS)], modes.at[CHANNELS + c], store_sem.at[1, c]),
             pltpu.make_async_copy(lower.at[c, pl.ds(1, ROWS)], modes.at[2 * CHANNELS + c], store_sem.at[2, c]),
-            pltpu.make_async_copy(left.at[c], modes.at[3 * CHANNELS + c], store_sem.at[3, c]),
+            pltpu.make_async_copy(
+                right.at[c, :, inner_cols, :], modes.at[3 * CHANNELS + c, :, outer_cols, :], store_sem.at[3, c]
+            ),
             pltpu.make_async_copy(right.at[c], modes.at[4 * CHANNELS + c], store_sem.at[4, c]),
         ]
 
+    first_store = pltpu.make_async_copy(
+        left, modes.at[pl.ds(3 * CHANNELS, CHANNELS), :, 0, :], load_sem.at[0]
+    )
+    left[...] = mixed(flat(first_column[...] * west[...])).reshape((CHANNELS, ROWS, LANES))
+    first_store.start()
+
     def channel(c, carry):
-        value = body[c, 1 : ROWS + 1, 8 : 8 + COLS, :]
-        shape = (ROWS, COLS, LANES)
-        plain[c] = mixed(flat(value)).reshape(shape)
-        pairs = body[c, 0 : ROWS + 1, 8 : 8 + COLS, :] * body[c, 1 : ROWS + 2, 8 : 8 + COLS, :]
-        lower[c] = mixed(flat(pairs)).reshape((ROWS + 1, COLS, LANES))
-        left[c] = mixed(flat(value * body[c, 1 : ROWS + 1, 7 : 7 + COLS, :])).reshape(shape)
-        right[c] = mixed(flat(value * body[c, 1 : ROWS + 1, 9 : 9 + COLS, :])).reshape(shape)
+        value = body[c, 1 : ROWS + 1, 0:COLS, :]
+        pairs = body[c, 0 : ROWS + 1, 0:COLS, :] * body[c, 1 : ROWS + 2, 0:COLS, :]
+        beside = value * body[c, 1 : ROWS + 1, 1 : COLS + 1, :]
+        both = mixed(jnp.concatenate([flat(value), flat(pairs), flat(beside)], axis=0))
+        cells = ROWS * COLS
+        plain[c] = both[:cells].reshape((ROWS, COLS, LANES))
+        lower[c] = both[cells : 2 * cells + COLS].reshape((ROWS + 1, COLS, LANES))
+        right[c] = both[2 * cells + COLS :].reshape((ROWS, COLS, LANES))
         for copy in stores(c):
             copy.start()
         return carry
 
-    lax.fori_loop(0, CHANNELS, channel, 0)
+    lax.fori_loop(0, CHANNELS, channel, 0, unroll=True)
 
     shifted = jnp.where(lane == LANES - 1, extended, pltpu.roll(factor, LANES - 1, 1))
     forward[...] = accurate(shifted, inverse)
@@ -532,6 +551,7 @@
         return carry
 
     lax.fori_loop(0, CHANNELS, finish, 0)
+    first_store.wait()
 
 
 def modes_call(fields, gram, north, south, west, east):
@@ -545,28 +565,29 @@
             jax.ShapeDtypeStruct((LANES, LANES), F32),
             jax.ShapeDtypeStruct((LANES, LANES), F32),
         ],
-        in_specs=[pl.BlockSpec(memory_space=pltpu.HBM), vmem, any_space, any_space, any_space, any_space],
+        in_specs=[pl.BlockSpec(memory_space=pltpu.HBM), vmem, any_space, any_space, vmem, any_space],
         out_specs=[any_space, vmem, vmem],
         scratch_shapes=[
-            pltpu.VMEM((CHANNELS, ROWS + 2, COLS + 16, LANES), F32),
+            pltpu.VMEM((CHANNELS, ROWS + 2, COLS + 8, LANES), F32),
             pltpu.VMEM((LANES // 8, 8, 2 * LANES), F32),
             pltpu.VMEM((LANES // 8, 8, 2 * LANES), F32),
             pltpu.VMEM((8, 8, LANES), F32),
             pltpu.VMEM((8, 8, LANES), F32),
             pltpu.VMEM((2 * LANES, 2 * LANES), BF16),
+            pltpu.VMEM((CHANNELS, ROWS, LANES), F32),
             pltpu.VMEM(shape, F32),
             pltpu.VMEM((CHANNELS, ROWS + 1, COLS, LANES), F32),
-            pltpu.VMEM(shape, F32),
+            pltpu.VMEM((CHANNELS, ROWS, LANES), F32),
             pltpu.VMEM(shape, F32),
             pltpu.SemaphoreType.DMA((5,)),
             pltpu.SemaphoreType.DMA((5, CHANNELS)),
         ],
-        compiler_params=pltpu.CompilerParams(vmem_limit_bytes=64_500_000),
+        compiler_params=pltpu.CompilerParams(vmem_limit_bytes=48 << 20),
     )(fields, gram, north, south, west, east)
 
 
 def shards(fields):
-    cells = fields.transpose(1, 2, 3, 0)
+    cells = pltpu.with_memory_space_constraint(fields.transpose(1, 2, 3, 0), pltpu.HBM)
     gram, north, south, west, east = gram_call(cells, lax.axis_size("lat"), lax.axis_size("lon"))
     return tuple(modes_call(cells, gram, north, south, west, east))
 

time: 44.8 us -> 42.7 us (0.953)
  Pallas kernels: 44 us -> 42 us
    pallas_call x1, Pallas kernels: 13.6 us -> 12.3 us  [modes_call(): pl.pallas_call(modes_kernel, out_shape=[jax.ShapeDtypeStruct((5 * CHANNEL...]
    pallas_call x1, Pallas kernels: 30.4 us -> 29.7 us  [gram_call(): pl.pallas_call(functools.partial(gram_kernel, (n_lat, n_y, n_z), cells_to...]
where the time goes in v4:
time: 42.7 us; the launch traced here: 42.6 us
  Pallas kernels  42 us (98%)
  between operations  0.64 us (1%)
    pallas_call x1, Pallas kernels, gram_call(): pl.pallas_call(functools.partial(gram_kernel, (n_lat, n_y, n_z), cells_to...  29.7 us
    pallas_call x1, Pallas kernels, modes_call(): pl.pallas_call(modes_kernel, out_shape=[jax.ShapeDtypeStruct((5 * CHANNEL...  12.3 us

profile of v4, /device:TPU:1, one launch (start us, length us, event | category | flops | bytes accessed | tf_op | source)
XLA Modules:
  0.0 42.6 jit_solution(8070930523990862872)
XLA Ops:
  0.6 29.7 %shard_map.38 = (f32[8,9,128]{2,1,0:T(8,128)S(1)}, f32[6,32,128]{2,1,0:T(8,128)S(1)}, f32[6,32,128]{2,1,0:T(8,128)S(1)}, f32[6,16,128]{2,1,0:T(8,128)S(1)}, f32[6,16,128]{2,1,0:T(8,128)S(1)}) custom-call(f32[6,16,32,129]{3,2,1,0:T(8,128)} %bitcast.1), custom_call_target="tpu_custom_call" | custom-call | tf_op jit(solution)/shard_map/pallas_call | solution.py:328
  30.3 12.3 %shard_map.39 = (f32[30,16,32,128]{3,2,1,0:T(8,128)}, f32[128,128]{1,0:T(8,128)}, f32[128,128]{1,0:T(8,128)}) custom-call(f32[6,16,32,129]{3,2,1,0:T(8,128)} %bitcast.2, f32[8,9,128]{2,1,0:T(8,128)S(1)} %get-tuple-element.8.gram, f32[6,32,128]{2,1,0:T(8,128)S(1)} %get-tuple-element.9.north, f32[6,32,128]{2,1,0:T(8,128)S(1)} %get-tuple-element.10.south, ...), custom_call_target="tpu_custom_call" | custom-call | tf_op jit(solution)/shard_map/pallas_call | solution.py:561

commit v5 on v4

--- a/solution.py
+++ b/solution.py
@@ -35,9 +35,18 @@
     rest = value - high.astype(F32)
     pair = jnp.concatenate([high, rest.astype(BF16)], axis=-1)
     turned = high.T
+    squares = pair[:, LANES:] * pair[:, LANES:]
+    squares = squares.reshape(-1, 16, LANES)
+    count = squares.shape[0]
+    total = jnp.zeros((8, LANES), F32)
+    for first in range(0, count, 8):
+        group = [squares[index] for index in range(first, min(first + 8, count))]
+        while len(group) > 1:
+            group = [left + right for left, right in zip(group[::2], group[1::2])] + group[len(group) // 2 * 2 :]
+        total += group[0].astype(F32).reshape(2, 8, LANES).sum(axis=0)
     if tails is not None:
         turned = jnp.concatenate([turned, tails], axis=0)
-    return jnp.dot(turned, pair, preferred_element_type=F32), sums(rest, rest)
+    return jnp.dot(turned, pair, preferred_element_type=F32), total
 
 
 def gram_kernel(
@@ -64,6 +73,26 @@
     def z_peer(step):
         return (z + step) % n_z
 
+    main = pl.ds(0, LANES)
+
+    def load(c):
+        return pltpu.make_async_copy(
+            fields.at[c, :, :, main], body.at[c, pl.ds(0, ROWS), pl.ds(0, COLS), :], load_sem.at[c]
+        )
+
+    tail_load = pltpu.make_async_copy(
+        fields.at[:, :, :, pl.ds(LANES, 1)], last, tail_sem.at[0]
+    )
+    edge_load = pltpu.make_async_copy(fields.at[:, :, COLS - 1, main], edge, tail_sem.at[1])
+    tail_load.start()
+
+    def start_load(c, carry):
+        load(c).start()
+        return carry
+
+    lax.fori_loop(0, CHANNELS, start_load, 0)
+    edge_load.start()
+
     barrier = pltpu.get_barrier_semaphore()
     greeted = [west_id, east_id]
     greeted += [{"lat": lat_peer(step)} for step in range(1, n_lat)]
@@ -71,26 +100,6 @@
     greeted += [{"lon": y * n_z + z_peer(step)} for step in range(1, n_z)]
     for peer in greeted:
         pl.semaphore_signal(barrier, inc=1, device_id=peer, device_id_type=MESH)
-
-    main = pl.ds(0, LANES)
-
-    def load(c):
-        return pltpu.make_async_copy(
-            fields.at[c, :, :, main], body.at[c, pl.ds(0, ROWS), pl.ds(0, COLS), :], load_sem.at[c]
-        )
-
-    tail_load = pltpu.make_async_copy(
-        fields.at[:, :, :, pl.ds(LANES, 1)], last, tail_sem.at[0]
-    )
-    edge_load = pltpu.make_async_copy(fields.at[:, :, COLS - 1, main], edge, tail_sem.at[1])
-    tail_load.start()
-
-    def start_load(c, carry):
-        load(c).start()
-        return carry
-
-    lax.fori_loop(0, CHANNELS, start_load, 0)
-    edge_load.start()
 
     pl.semaphore_wait(barrier, len(greeted))
     def remote(source, target, index, peer):
@@ -258,14 +267,20 @@
         part[owner, rows : rows + 1, :] = tail
 
     def exchange(count, me, peer_of, device_of, source_of, buf, send, recv):
-        def start(step, carry):
+        def start(step):
             peer = peer_of(step)
             pltpu.make_async_remote_copy(
                 source_of(peer), buf.at[me], send.at[0], recv.at[0], device_id=device_of(peer), device_id_type=MESH
             ).start()
+
+        start(count // 2)
+
+        def start_two(t, carry):
+            start(count // 2 + t)
+            start(count // 2 - t)
             return carry
 
-        lax.fori_loop(1, count, start, 0)
+        lax.fori_loop(1, count // 2, start_two, 0)
         others = buf.at[pl.ds(0, count - 1)]
         pltpu.make_async_copy(others, others, recv.at[0]).wait()
         return pltpu.make_async_copy(others, others, send.at[0])
@@ -398,24 +413,48 @@
     return one, two, value - one - two
 
 
-def eliminate(b, works, splats, first_row):
+def eliminate(b, works, splats, nears, turned_refs, done_refs, first_row):
     start = b * 8
     sub, lane = iota((8, LANES), 0), iota((8, LANES), 1)
     upper = sub < 4
-    for work, columns in zip(works, splats):
-        block = pltpu.roll(work[b, :, 0:LANES], (LANES - start) % LANES, 1)
-        for j in range(8):
-            columns[j] = jnp.broadcast_to(block[:, j : j + 1], (8, LANES))
-
-    def paired(first, second):
+    left_part, right_part = slice(0, LANES), slice(LANES, 2 * LANES)
+    after = lax.min(b + 1, LANES // 8 - 1)
+
+    def joined(first, second):
+        return [jnp.where(upper, first, pltpu.roll(second, 4, 0)), jnp.where(upper, pltpu.roll(first, 4, 0), second)]
+
+    following = []
+    for work, turned, done in zip(works, turned_refs, done_refs):
+        small = jnp.dot(turned[after].astype(BF16), done[...], preferred_element_type=F32)
+        following.append(work[after] - small)
+    below = slice(first_row // 8, LANES // 8)
+    for work, turned, done in zip(works, turned_refs, done_refs):
+        update = jnp.dot(flat(turned[below]).astype(BF16), done[...], preferred_element_type=F32)
+        work[below] = work[below] - update.reshape(-1, 8, 2 * LANES)
+    next_left = joined(*[rows[:, left_part] for rows in following])
+    next_right = joined(*[rows[:, right_part] for rows in following])
+
+    shift = (LANES - start) % LANES
+
+    def columns_of(rows, first):
+        block = pltpu.roll(rows, shift, 1)
+        return {j: jnp.broadcast_to(block[:, j : j + 1], (8, LANES)) for j in range(first, 8)}
+
+    for h in range(2):
+        for j, column in columns_of(nears[h, :, left_part], 4 * h).items():
+            splats[h, j] = column
+
+    def paired(ref, row):
+        first, second = ref[row : row + 1, :], ref[4 + row : 5 + row, :]
         return jnp.where(upper, jnp.broadcast_to(first, (8, LANES)), jnp.broadcast_to(second, (8, LANES)))
 
     entry = {}
     for i in range(8):
         for j in range(i, 8):
-            entry[i, j] = paired(*[columns[j, i : i + 1, :] for columns in splats])
-    left_rows = [paired(*[work[b, i : i + 1, 0:LANES] for work in works]) for i in range(8)]
-    right_rows = [paired(*[work[b, i : i + 1, LANES : 2 * LANES] for work in works]) for i in range(8)]
+            entry[i, j] = paired(splats.at[i // 4, j], i % 4)
+    left_rows = [paired(nears.at[i // 4, :, left_part], i % 4) for i in range(8)]
+    right_rows = [paired(nears.at[i // 4, :, right_part], i % 4) for i in range(8)]
+    next_columns = [columns_of(rows, 0) for rows in next_left]
     inverse = []
     for k in range(8):
         inverse.append(1.0 / entry[k, k])
@@ -425,27 +464,33 @@
                 entry[i, j] = entry[i, j] - factor * entry[k, j]
             left_rows[i] = left_rows[i] - factor * left_rows[k]
             right_rows[i] = right_rows[i] - factor * right_rows[k]
+        for h in range(2):
+            factor = next_columns[h][k] * inverse[k]
+            for j in range(k + 1, 8):
+                next_columns[h][j] = next_columns[h][j] - factor * entry[k, j]
+            next_left[h] = next_left[h] - factor * left_rows[k]
+            next_right[h] = next_right[h] - factor * right_rows[k]
+    for h in range(2):
+        nears[h, :, left_part] = next_left[h]
+        nears[h, :, right_part] = next_right[h]
 
     def gathered(rows):
         low, high = rows[0], rows[4]
         for k in range(1, 4):
             low = jnp.where(sub % 4 == k, rows[k], low)
             high = jnp.where(sub % 4 == k, rows[4 + k], high)
-        return jnp.where(upper, low, pltpu.roll(high, 4, 0)), jnp.where(upper, pltpu.roll(low, 4, 0), high)
-
-    below = slice(first_row // 8, LANES // 8)
-    for work, pivots, done_left, done_right in zip(
-        works, gathered(inverse), gathered(left_rows), gathered(right_rows)
+        return joined(low, high)
+
+    for work, turned, done, pivots, done_left, done_right in zip(
+        works, turned_refs, done_refs, gathered(inverse), gathered(left_rows), gathered(right_rows)
     ):
-        f1, f2, f3 = split_three(jnp.where(lane >= start + 8, done_left * pivots, 0.0))
+        f1, f2, f3 = split_three(jnp.where(lane >= start + 16, done_left * pivots, 0.0))
         d1, d2, d3 = split_three(jnp.concatenate([done_left, done_right], axis=1))
-        factors = jnp.concatenate([f1, f1, f2, f1, f2, f3], axis=0).T.astype(BF16)
-        done = jnp.concatenate([d1, d2, d1, d3, d2, d1], axis=0).astype(BF16)
-        update = jnp.dot(factors[first_row:], done, preferred_element_type=F32)
+        turned[...] = jnp.concatenate([f1, f1, f2, f1, f2, f3], axis=0).T.reshape(-1, 8, 48)
+        done[...] = jnp.concatenate([d1, d2, d1, d3, d2, d1], axis=0).astype(BF16)
         root = jnp.sqrt(pivots)
-        work[b, :, 0:LANES] = done_left * root
-        work[b, :, LANES : 2 * LANES] = done_right * root
-        work[below] = work[below] - update.reshape(-1, 8, 2 * LANES)
+        work[b, :, left_part] = done_left * root
+        work[b, :, right_part] = done_right * root
 
 
 def accurate(left, right):
@@ -456,10 +501,10 @@
 
 def modes_kernel(
     fields, gram, north, south, west, east, modes, forward, backward,
-    body, work_one, work_two, splat_one, splat_two, weights, first_column, plain, lower, left, right,
+    body, work_one, work_two, splat, near, turned_one, turned_two, done_one, done_two, weights, first_column, plain, lower, left, right,
     load_sem, store_sem,
 ):
-    works, splats = (work_one, work_two), (splat_one, splat_two)
+    works, turned, done = (work_one, work_two), (turned_one, turned_two), (done_one, done_two)
     main = pl.ds(0, LANES)
     inner = pl.ds(1, ROWS)
     loads = [
@@ -476,10 +521,18 @@
         work[:, :, 0:LANES] = matrix.reshape(-1, 8, LANES)
         work[:, :, LANES : 2 * LANES] = extended.reshape(-1, 8, LANES)
 
+    upper = iota((8, LANES), 0) < 4
+    for part in range(0, 2 * LANES, LANES):
+        first, second = [work[0, :, part : part + LANES] for work in works]
+        near[0, :, part : part + LANES] = jnp.where(upper, first, pltpu.roll(second, 4, 0))
+        near[1, :, part : part + LANES] = jnp.where(upper, pltpu.roll(first, 4, 0), second)
+    for ref in turned + done:
+        ref[...] = jnp.zeros_like(ref)
+
     for phase in range(4):
 
         def step(b, carry):
-            eliminate(b, works, splats, phase * 32)
+            eliminate(b, works, splat, near, turned, done, phase * 32)
             return carry
 
         lax.fori_loop(phase * 4, phase * 4 + 4, step, 0)
@@ -571,8 +624,12 @@
             pltpu.VMEM((CHANNELS, ROWS + 2, COLS + 8, LANES), F32),
             pltpu.VMEM((LANES // 8, 8, 2 * LANES), F32),
             pltpu.VMEM((LANES // 8, 8, 2 * LANES), F32),
-            pltpu.VMEM((8, 8, LANES), F32),
-            pltpu.VMEM((8, 8, LANES), F32),
+            pltpu.VMEM((2, 8, 8, LANES), F32),
+            pltpu.VMEM((2, 8, 2 * LANES), F32),
+            pltpu.VMEM((LANES // 8, 8, 48), F32),
+            pltpu.VMEM((LANES // 8, 8, 48), F32),
+            pltpu.VMEM((48, 2 * LANES), BF16),
+            pltpu.VMEM((48, 2 * LANES), BF16),
             pltpu.VMEM((2 * LANES, 2 * LANES), BF16),
             pltpu.VMEM((CHANNELS, ROWS, LANES), F32),
             pltpu.VMEM(shape, F32),

time: 42.7 us -> 40.8 us (0.956)
  Pallas kernels: 42 us -> 40.1 us
    pallas_call x1, Pallas kernels: 12.3 us -> 10.4 us  [modes_call(): pl.pallas_call(modes_kernel, out_shape=[jax.ShapeDtypeStruct((5 * CHANNEL...]
where the time goes in v5:
time: 40.8 us
  Pallas kernels  40.1 us (98%)
  between operations  0.64 us (2%)
    pallas_call x1, Pallas kernels, gram_call(): pl.pallas_call(functools.partial(gram_kernel, (n_lat, n_y, n_z), cells_to...  29.7 us
    pallas_call x1, Pallas kernels, modes_call(): pl.pallas_call(modes_kernel, out_shape=[jax.ShapeDtypeStruct((5 * CHANNEL...  10.4 us

profile of v5, /device:TPU:1, one launch (start us, length us, event | category | flops | bytes accessed | tf_op | source)
XLA Modules:
  0.0 40.8 jit_solution(9229319283489502798)
XLA Ops:
  0.6 29.7 %shard_map.38 = (f32[8,9,128]{2,1,0:T(8,128)S(1)}, f32[6,32,128]{2,1,0:T(8,128)S(1)}, f32[6,32,128]{2,1,0:T(8,128)S(1)}, f32[6,16,128]{2,1,0:T(8,128)S(1)}, f32[6,16,128]{2,1,0:T(8,128)S(1)}) custom-call(f32[6,16,32,129]{3,2,1,0:T(8,128)} %bitcast.1), custom_call_target="tpu_custom_call" | custom-call | tf_op jit(solution)/shard_map/pallas_call | solution.py:343
  30.3 10.4 %shard_map.39 = (f32[30,16,32,128]{3,2,1,0:T(8,128)}, f32[128,128]{1,0:T(8,128)}, f32[128,128]{1,0:T(8,128)}) custom-call(f32[6,16,32,129]{3,2,1,0:T(8,128)} %bitcast.2, f32[8,9,128]{2,1,0:T(8,128)S(1)} %get-tuple-element.8.gram, f32[6,32,128]{2,1,0:T(8,128)S(1)} %get-tuple-element.9.north, f32[6,32,128]{2,1,0:T(8,128)S(1)} %get-tuple-element.10.south, ...), custom_call_target="tpu_custom_call" | custom-call | tf_op jit(solution)/shard_map/pallas_call | solution.py:614

commit v6 on v5

--- a/solution.py
+++ b/solution.py
@@ -55,7 +55,7 @@
     body, last, edge, north, south, west, east,
     pack_row, pack_col, got_row, got_col, tail_cells, tails_ref,
     acc_one, acc_two, part, lat_buf, y_buf, z_buf, all_buf,
-    load_sem, tail_sem, halo_send, halo_recv, lat_send, lat_recv, y_send, y_recv, z_send, z_recv, all_send, all_recv,
+    relay_sem, load_sem, tail_sem, halo_send, halo_recv, lat_send, lat_recv, y_send, y_recv, z_send, z_recv, all_send, all_recv,
 ):
     n_lat, n_y, n_z = sizes
     n_lon = n_y * n_z
@@ -97,40 +97,9 @@
     greeted = [west_id, east_id]
     greeted += [{"lat": lat_peer(step)} for step in range(1, n_lat)]
     greeted += [{"lon": y_peer(step) * n_z + z} for step in range(1, n_y)]
-    greeted += [{"lon": y * n_z + z_peer(step)} for step in range(1, n_z)]
+    greeted += [{"lon": y * n_z + z_peer(step)} for step in range(1, n_z) if min(step, n_z - step) <= 2]
     for peer in greeted:
         pl.semaphore_signal(barrier, inc=1, device_id=peer, device_id_type=MESH)
-
-    pl.semaphore_wait(barrier, len(greeted))
-    def remote(source, target, index, peer):
-        return pltpu.make_async_remote_copy(
-            source, target, halo_send.at[index], halo_recv.at[index], device_id=peer, device_id_type=MESH
-        )
-
-    lat_up = {"lat": lax.max(lat - 1, 0)}
-    lat_down = {"lat": lax.min(lat + 1, n_lat - 1)}
-    east_copies = [
-        remote(fields.at[:, :, 0, main], east, 0, west_id),
-        remote(pack_col, got_col, 1, west_id),
-    ]
-    south_copies = [
-        remote(fields.at[:, 0, :, main], south, 2, lat_up),
-        remote(pack_row, got_row, 3, lat_up),
-    ]
-    west_copy = remote(fields.at[:, :, COLS - 1, main], west, 4, east_id)
-    north_copy = remote(fields.at[:, ROWS - 1, :, main], north, 5, lat_down)
-
-    @pl.when(lat > 0)
-    def _():
-        south_copies[0].start()
-
-    east_copies[0].start()
-
-    @pl.when(lat < n_lat - 1)
-    def _():
-        north_copy.start()
-
-    west_copy.start()
 
     body[:, ROWS : ROWS + 1, 0:COLS, :] = jnp.zeros((CHANNELS, 1, COLS, LANES), F32)
     body[:, :, COLS : COLS + 8, :] = jnp.zeros((CHANNELS, ROWS + 1, 8, LANES), F32)
@@ -156,12 +125,6 @@
         return result
 
     pack_col[...] = column(tail_cells, 0)
-    east_copies[1].start()
-
-    @pl.when(lat > 0)
-    def _():
-        south_copies[1].start()
-
     count = 4 * CHANNELS
     tail = merged.T[:count]
     row, lane = iota((count, LANES), 0), iota((count, LANES), 1)
@@ -184,6 +147,40 @@
     own_one = sums(tail, tail)
     own_two = sums(lower, lower) + sums(right, right)
 
+    pl.semaphore_wait(barrier, len(greeted))
+    relayed = n_z > 5
+    if relayed:
+        for step in (2, n_z - 2):
+            pl.semaphore_signal(
+                relay_sem, inc=1, device_id={"lon": y * n_z + z_peer(step)}, device_id_type=MESH
+            )
+
+    def remote(source, target, index, peer):
+        return pltpu.make_async_remote_copy(
+            source, target, halo_send.at[index], halo_recv.at[index], device_id=peer, device_id_type=MESH
+        )
+
+    lat_up = {"lat": lax.max(lat - 1, 0)}
+    lat_down = {"lat": lax.min(lat + 1, n_lat - 1)}
+    east_copies = [
+        remote(fields.at[:, :, 0, main], east, 0, west_id),
+        remote(pack_col, got_col, 1, west_id),
+    ]
+    south_copies = [
+        remote(fields.at[:, 0, :, main], south, 2, lat_up),
+        remote(pack_row, got_row, 3, lat_up),
+    ]
+    west_copy = remote(fields.at[:, :, COLS - 1, main], west, 4, east_id)
+    north_copy = remote(fields.at[:, ROWS - 1, :, main], north, 5, lat_down)
+
+    @pl.when(lat > 0)
+    def _():
+        for copy in south_copies:
+            copy.start()
+
+    for copy in east_copies:
+        copy.start()
+
     zero = jnp.zeros((8, LANES), F32)
 
     def channel(c, carry):
@@ -211,6 +208,12 @@
 
     for copy in east_copies:
         copy.wait_recv()
+
+    @pl.when(lat < n_lat - 1)
+    def _():
+        north_copy.start()
+
+    west_copy.start()
 
     @pl.when(lat == n_lat - 1)
     def _():
@@ -300,6 +303,8 @@
         n_y, y, y_peer, lambda p: {"lon": p * n_z + z}, lambda p: y_buf.at[y], y_buf, y_send, y_recv
     )]
     z_buf[z] = added(y_buf, n_y)
+    if relayed:
+        pl.semaphore_wait(relay_sem, 2)
     pending += [exchange(
         n_z, z, z_peer, lambda p: {"lon": y * n_z + p}, lambda p: z_buf.at[z], z_buf, z_send, z_recv
     )]
@@ -363,6 +368,7 @@
             pltpu.VMEM((n_y,) + chunk, F32),
             pltpu.VMEM((n_z,) + chunk, F32),
             pltpu.VMEM((n_lat,) + chunk, F32),
+            pltpu.SemaphoreType.REGULAR,
             dma((CHANNELS,)), dma((2,)),
             dma((6,)), dma((6,)),
             dma((1,)), dma((1,)),
@@ -501,7 +507,7 @@
 
 def modes_kernel(
     fields, gram, north, south, west, east, modes, forward, backward,
-    body, work_one, work_two, splat, near, turned_one, turned_two, done_one, done_two, weights, first_column, plain, lower, left, right,
+    body, work_one, work_two, splat, near, turned_one, turned_two, done_one, done_two, weights, first_column, plain, lower, left, right, operators,
     load_sem, store_sem,
 ):
     works, turned, done = (work_one, work_two), (turned_one, turned_two), (done_one, done_two)
@@ -561,15 +567,20 @@
     inner_cols, outer_cols = pl.ds(0, COLS - 1), pl.ds(1, COLS - 1)
 
     def stores(c):
-        return [
-            pltpu.make_async_copy(plain.at[c], modes.at[c], store_sem.at[0, c]),
-            pltpu.make_async_copy(lower.at[c, pl.ds(0, ROWS)], modes.at[CHANNELS + c], store_sem.at[1, c]),
-            pltpu.make_async_copy(lower.at[c, pl.ds(1, ROWS)], modes.at[2 * CHANNELS + c], store_sem.at[2, c]),
-            pltpu.make_async_copy(
-                right.at[c, :, inner_cols, :], modes.at[3 * CHANNELS + c, :, outer_cols, :], store_sem.at[3, c]
-            ),
-            pltpu.make_async_copy(right.at[c], modes.at[4 * CHANNELS + c], store_sem.at[4, c]),
-        ]
+        pieces = (
+            (plain.at[c], modes.at[c]),
+            (lower.at[c, pl.ds(0, ROWS)], modes.at[CHANNELS + c]),
+            (lower.at[c, pl.ds(1, ROWS)], modes.at[2 * CHANNELS + c]),
+            (right.at[c, :, inner_cols, :], modes.at[3 * CHANNELS + c, :, outer_cols, :]),
+            (right.at[c], modes.at[4 * CHANNELS + c]),
+        )
+        return [pltpu.make_async_copy(*piece, store_sem.at[kind]) for kind, piece in enumerate(pieces)]
+
+    def stored(kind):
+        whole = modes.at[pl.ds(kind * CHANNELS, CHANNELS)]
+        if kind == 3:
+            whole = whole.at[:, :, outer_cols, :]
+        return pltpu.make_async_copy(whole, whole, store_sem.at[kind])
 
     first_store = pltpu.make_async_copy(
         left, modes.at[pl.ds(3 * CHANNELS, CHANNELS), :, 0, :], load_sem.at[0]
@@ -593,18 +604,19 @@
     lax.fori_loop(0, CHANNELS, channel, 0, unroll=True)
 
     shifted = jnp.where(lane == LANES - 1, extended, pltpu.roll(factor, LANES - 1, 1))
-    forward[...] = accurate(shifted, inverse)
+    operators[0] = accurate(shifted, inverse)
+    forward_store = pltpu.make_async_copy(operators.at[0], forward, load_sem.at[1])
+    forward_store.start()
     factor, extended, inverse = parts(1)
     mixed_block = jnp.where(lane == 0, pltpu.roll(extended, 1, 1), pltpu.roll(factor, 1, 1))
-    backward[...] = accurate(mixed_block, inverse)
-
-    def finish(c, carry):
-        for copy in stores(c):
-            copy.wait()
-        return carry
-
-    lax.fori_loop(0, CHANNELS, finish, 0)
+    operators[1] = accurate(mixed_block, inverse)
+    backward_store = pltpu.make_async_copy(operators.at[1], backward, load_sem.at[2])
+    backward_store.start()
+    for kind in range(5):
+        stored(kind).wait()
     first_store.wait()
+    forward_store.wait()
+    backward_store.wait()
 
 
 def modes_call(fields, gram, north, south, west, east):
@@ -619,7 +631,7 @@
             jax.ShapeDtypeStruct((LANES, LANES), F32),
         ],
         in_specs=[pl.BlockSpec(memory_space=pltpu.HBM), vmem, any_space, any_space, vmem, any_space],
-        out_specs=[any_space, vmem, vmem],
+        out_specs=[any_space] * 3,
         scratch_shapes=[
             pltpu.VMEM((CHANNELS, ROWS + 2, COLS + 8, LANES), F32),
             pltpu.VMEM((LANES // 8, 8, 2 * LANES), F32),
@@ -636,8 +648,9 @@
             pltpu.VMEM((CHANNELS, ROWS + 1, COLS, LANES), F32),
             pltpu.VMEM((CHANNELS, ROWS, LANES), F32),
             pltpu.VMEM(shape, F32),
+            pltpu.VMEM((2, LANES, LANES), F32),
             pltpu.SemaphoreType.DMA((5,)),
-            pltpu.SemaphoreType.DMA((5, CHANNELS)),
+            pltpu.SemaphoreType.DMA((5,)),
         ],
         compiler_params=pltpu.CompilerParams(vmem_limit_bytes=48 << 20),
     )(fields, gram, north, south, west, east)

time: 40.8 us -> 39.8 us (0.975)
  Pallas kernels: 40.1 us -> 39 us
    pallas_call x1, Pallas kernels: 10.4 us -> 9.58 us  [modes_call(): pl.pallas_call(modes_kernel, out_shape=[jax.ShapeDtypeStruct((5 * CHANNEL...]
where the time goes in v6:
time: 39.8 us; the launch traced here: 39.7 us
  Pallas kernels  39 us (98%)
  between operations  0.64 us (2%)
    pallas_call x1, Pallas kernels, gram_call(): pl.pallas_call(functools.partial(gram_kernel, (n_lat, n_y, n_z), cells_to...  29.5 us
    pallas_call x1, Pallas kernels, modes_call(): pl.pallas_call(modes_kernel, out_shape=[jax.ShapeDtypeStruct((5 * CHANNEL...  9.58 us

profile of v6, /device:TPU:1, one launch (start us, length us, event | category | flops | bytes accessed | tf_op | source)
XLA Modules:
  0.0 39.7 jit_solution(7393601249641966571)
XLA Ops:
  0.6 29.5 %shard_map.38 = (f32[8,9,128]{2,1,0:T(8,128)S(1)}, f32[6,32,128]{2,1,0:T(8,128)S(1)}, f32[6,32,128]{2,1,0:T(8,128)S(1)}, f32[6,16,128]{2,1,0:T(8,128)S(1)}, f32[6,16,128]{2,1,0:T(8,128)S(1)}) custom-call(f32[6,16,32,129]{3,2,1,0:T(8,128)} %bitcast.1), custom_call_target="tpu_custom_call" | custom-call | tf_op jit(solution)/shard_map/pallas_call | solution.py:348
  30.1 9.6 %shard_map.39 = (f32[30,16,32,128]{3,2,1,0:T(8,128)}, f32[128,128]{1,0:T(8,128)}, f32[128,128]{1,0:T(8,128)}) custom-call(f32[6,16,32,129]{3,2,1,0:T(8,128)} %bitcast.2, f32[8,9,128]{2,1,0:T(8,128)S(1)} %get-tuple-element.8.gram, f32[6,32,128]{2,1,0:T(8,128)S(1)} %get-tuple-element.9.north, f32[6,32,128]{2,1,0:T(8,128)S(1)} %get-tuple-element.10.south, ...), custom_call_target="tpu_custom_call" | custom-call | tf_op jit(solution)/shard_map/pallas_call | solution.py:626

commit v7 on v6

--- a/solution.py
+++ b/solution.py
@@ -269,7 +269,7 @@
         tail = cross if owner == 0 else extra if owner == 1 else jnp.zeros((1, LANES), F32)
         part[owner, rows : rows + 1, :] = tail
 
-    def exchange(count, me, peer_of, device_of, source_of, buf, send, recv):
+    def exchange(count, me, peer_of, device_of, source_of, buf, send, recv, meanwhile=None):
         def start(step):
             peer = peer_of(step)
             pltpu.make_async_remote_copy(
@@ -284,6 +284,8 @@
             return carry
 
         lax.fori_loop(1, count // 2, start_two, 0)
+        if meanwhile is not None:
+            meanwhile()
         others = buf.at[pl.ds(0, count - 1)]
         pltpu.make_async_copy(others, others, recv.at[0]).wait()
         return pltpu.make_async_copy(others, others, send.at[0])
@@ -293,6 +295,25 @@
         for index in range(1, count):
             result = result + buf[index]
         return result
+
+    def finish_borders():
+        @pl.when(lat > 0)
+        def _():
+            north_copy.wait_recv()
+            for copy in south_copies:
+                copy.wait_send()
+
+        @pl.when(lat < n_lat - 1)
+        def _():
+            north_copy.wait_send()
+
+        west_copy.wait_recv()
+        for copy in [west_copy] + east_copies:
+            copy.wait_send()
+        north_out[...] = north[...]
+        south_out[...] = south[...]
+        west_out[...] = west[...]
+        east_out[...] = east[...]
 
     lat_buf[lat] = part[lat]
     pending = [exchange(
@@ -310,29 +331,13 @@
     )]
     all_buf[lat] = added(z_buf, n_z)
     pending += [exchange(
-        n_lat, lat, lat_peer, lambda p: {"lat": p}, lambda p: all_buf.at[lat], all_buf, all_send, all_recv
+        n_lat, lat, lat_peer, lambda p: {"lat": p}, lambda p: all_buf.at[lat], all_buf, all_send, all_recv,
+        finish_borders,
     )]
     gram_out[...] = all_buf[...]
 
-    @pl.when(lat > 0)
-    def _():
-        north_copy.wait_recv()
-        for copy in south_copies:
-            copy.wait_send()
-
-    @pl.when(lat < n_lat - 1)
-    def _():
-        north_copy.wait_send()
-
-    west_copy.wait_recv()
-    for copy in [west_copy] + east_copies:
-        copy.wait_send()
     for copy in pending:
         copy.wait()
-    north_out[...] = north[...]
-    south_out[...] = south[...]
-    west_out[...] = west[...]
-    east_out[...] = east[...]
 
 
 def gram_call(fields, n_lat, n_lon):
@@ -585,23 +590,25 @@
     first_store = pltpu.make_async_copy(
         left, modes.at[pl.ds(3 * CHANNELS, CHANNELS), :, 0, :], load_sem.at[0]
     )
-    left[...] = mixed(flat(first_column[...] * west[...])).reshape((CHANNELS, ROWS, LANES))
-    first_store.start()
-
     def channel(c, carry):
         value = body[c, 1 : ROWS + 1, 0:COLS, :]
         pairs = body[c, 0 : ROWS + 1, 0:COLS, :] * body[c, 1 : ROWS + 2, 0:COLS, :]
         beside = value * body[c, 1 : ROWS + 1, 1 : COLS + 1, :]
-        both = mixed(jnp.concatenate([flat(value), flat(pairs), flat(beside)], axis=0))
-        cells = ROWS * COLS
-        plain[c] = both[:cells].reshape((ROWS, COLS, LANES))
-        lower[c] = both[cells : 2 * cells + COLS].reshape((ROWS + 1, COLS, LANES))
-        right[c] = both[2 * cells + COLS :].reshape((ROWS, COLS, LANES))
-        for copy in stores(c):
-            copy.start()
+        copies = stores(c)
+        plain[c] = mixed(flat(value)).reshape((ROWS, COLS, LANES))
+        copies[0].start()
+        lower[c] = mixed(flat(pairs)).reshape((ROWS + 1, COLS, LANES))
+        copies[1].start()
+        copies[2].start()
+        right[c] = mixed(flat(beside)).reshape((ROWS, COLS, LANES))
+        copies[3].start()
+        copies[4].start()
         return carry
 
     lax.fori_loop(0, CHANNELS, channel, 0, unroll=True)
+
+    left[...] = mixed(flat(first_column[...] * west[...])).reshape((CHANNELS, ROWS, LANES))
+    first_store.start()
 
     shifted = jnp.where(lane == LANES - 1, extended, pltpu.roll(factor, LANES - 1, 1))
     operators[0] = accurate(shifted, inverse)

time: 39.8 us -> 39.7 us (level)
  no operation moved by 1% of the time
where the time goes in v7:
time: 39.7 us; the launch traced here: 39.6 us
  Pallas kernels  39 us (98%)
  between operations  0.64 us (2%)
    pallas_call x1, Pallas kernels, gram_call(): pl.pallas_call(functools.partial(gram_kernel, (n_lat, n_y, n_z), cells_to...  29.4 us
    pallas_call x1, Pallas kernels, modes_call(): pl.pallas_call(modes_kernel, out_shape=[jax.ShapeDtypeStruct((5 * CHANNEL...  9.54 us

profile of v7, /device:TPU:1, one launch (start us, length us, event | category | flops | bytes accessed | tf_op | source)
XLA Modules:
  0.0 39.6 jit_solution(12684250780349187135)
XLA Ops:
  0.6 29.4 %shard_map.38 = (f32[8,9,128]{2,1,0:T(8,128)S(1)}, f32[6,32,128]{2,1,0:T(8,128)S(1)}, f32[6,32,128]{2,1,0:T(8,128)S(1)}, f32[6,16,128]{2,1,0:T(8,128)S(1)}, f32[6,16,128]{2,1,0:T(8,128)S(1)}) custom-call(f32[6,16,32,129]{3,2,1,0:T(8,128)} %bitcast.1), custom_call_target="tpu_custom_call" | custom-call | tf_op jit(solution)/shard_map/pallas_call | solution.py:353
  30.1 9.5 %shard_map.39 = (f32[30,16,32,128]{3,2,1,0:T(8,128)}, f32[128,128]{1,0:T(8,128)}, f32[128,128]{1,0:T(8,128)}) custom-call(f32[6,16,32,129]{3,2,1,0:T(8,128)} %bitcast.2, f32[8,9,128]{2,1,0:T(8,128)S(1)} %get-tuple-element.8.gram, f32[6,32,128]{2,1,0:T(8,128)S(1)} %get-tuple-element.9.north, f32[6,32,128]{2,1,0:T(8,128)S(1)} %get-tuple-element.10.south, ...), custom_call_target="tpu_custom_call" | custom-call | tf_op jit(solution)/shard_map/pallas_call | solution.py:633
